TPU v7x, 32 devices: a whole 2x2x4 slice. The times are simulated.
32 devices in a mesh: batch: 8 (over y, x, core), blk: 4 (over z).
Axes of the slice: x: 2, y: 2, z: 4, core: 2. Of those that a mesh axis runs over, the one named last changes fastest.
Arguments:
- hidden_in: bfloat16 [16, 1024, 1024], P('batch', 'blk'), may hold values from -6 to 6
- mask_index: int32 [16, 153], P('batch'), may hold values from 0 to 1023, as said below
- mask_count: int32 [16], P('batch'), may hold values from 76 to 153, as said below
- replacement: bfloat16 [16, 153, 1024], P('batch'), may hold values from -6 to 6
- out_grad: bfloat16 [16, 153, 1024], P('batch'), may hold values from -6 to 6
- w_qkv: bfloat16 [2, 1024, 3072], P(None, ('batch', 'blk')), may hold values from -0.1875 to 0.1875
- w_out: bfloat16 [2, 1024, 1024], P(None, ('batch', 'blk')), may hold values from -0.5 to 0.5
- w_up: bfloat16 [2, 1024, 4096], P(None, ('batch', 'blk')), may hold values from -0.1875 to 0.1875
- w_down: bfloat16 [2, 4096, 1024], P(None, ('batch', 'blk')), may hold values from -0.09375 to 0.09375
- biases: bfloat16 [2, 6, 1024], P(None, None, ('batch', 'blk')), may hold values from -1.1953125 to 1.1953125
- up_bias: bfloat16 [2, 4096], P(None, ('batch', 'blk')), may hold values from -1.1953125 to 1.1953125
- gains: bfloat16 [2, 2, 1024], P(None, None, ('batch', 'blk')), may hold values from 0.5 to 1.5
Outputs:
- output: bfloat16 [16, 1024, 1024], P('batch', 'blk')
- input_grad: float32 [16, 1024, 1024], P('batch', 'blk')
- grad_qkv: float32 [2, 1024, 3072], P(None, ('batch', 'blk'))
- grad_out: float32 [2, 1024, 1024], P(None, ('batch', 'blk'))
- grad_up: float32 [2, 1024, 4096], P(None, ('batch', 'blk'))
- grad_down: float32 [2, 4096, 1024], P(None, ('batch', 'blk'))
- grad_biases: float32 [2, 6, 1024], P(None, None, ('batch', 'blk'))
- grad_up_bias: float32 [2, 4096], P(None, ('batch', 'blk'))
- grad_gains: float32 [2, 2, 1024], P(None, None, ('batch', 'blk'))
Inputs may be any that keep to these rules, and one draw needn't show every extreme that they name: `mask_index`: in each row the entries are distinct positions of the sequence; the first mask_count entries are the masked ones, the rest are padding, and the masked ones include a position in every aligned block of 256 positions. `mask_count`: some sequence has exactly 153.
All inputs are finite; a program needn't handle non-finite values.
Results may differ from a plain program's by a relative error of at most 0.029.
Values may be sent and summed in bfloat16 or wider, within the bound.
A program may use at most 448 MiB of HBM per device.

v0:
```python
import jax
import jax.numpy as jnp
from jax import lax
from jax.sharding import PartitionSpec as P

HEADS = 16


NORM_EPS = 1e-12
SCORE_SCALE = 0.125


def norm_rows(values, gain, shift):
    center = values - jnp.mean(values, -1, keepdims=True)
    spread = jnp.mean(center * center, -1, keepdims=True)
    return center * lax.rsqrt(spread + NORM_EPS) * gain + shift


def gelu_exact(values):
    return 0.5 * values * (1.0 + jax.scipy.special.erf(values * 0.7071067811865476))


def forward_layer(inputs, fetched, head_shape):
    qkv_weight, out_weight, up_weight, down_weight, bias_rows, up_shift, gain_rows = fetched
    bias_rows = bias_rows.astype(jnp.float32)
    up_shift = up_shift.astype(jnp.float32)
    gain_rows = gain_rows.astype(jnp.float32)
    seq_count, block_len, head_count, head_dim = head_shape
    model_width = head_count * head_dim
    inputs_low = inputs.astype(jnp.bfloat16)
    project = jnp.einsum("sbd,de->sbe", inputs_low, qkv_weight, preferred_element_type=jnp.float32)
    query = (project[..., :model_width] + bias_rows[0]).astype(jnp.bfloat16).reshape(head_shape)
    keys = project[..., model_width : 2 * model_width].astype(jnp.bfloat16).reshape(head_shape)
    values = (
        (project[..., 2 * model_width :] + bias_rows[1]).astype(jnp.bfloat16).reshape(head_shape)
    )
    stat_shape = (seq_count, head_count, block_len)
    top_now = jnp.full(stat_shape, -1e30, jnp.float32)
    key_part = lax.all_gather(keys, "blk", axis=1, tiled=True)
    value_part = lax.all_gather(values, "blk", axis=1, tiled=True)
    scores = (
        jnp.einsum("sqhd,skhd->shqk", query, key_part, preferred_element_type=jnp.float32)
        * SCORE_SCALE
    )
    top_next = jnp.maximum(top_now, jnp.max(scores, -1))
    weights_now = jnp.exp(scores - top_next[..., None])
    total_next = jnp.sum(weights_now, -1)
    acc_next = jnp.einsum(
        "shqk,skhd->shqd",
        weights_now.astype(jnp.bfloat16),
        value_part,
        preferred_element_type=jnp.float32,
    )
    log_total = top_next + jnp.log(total_next)
    attended = (acc_next / total_next[..., None]).transpose(0, 2, 1, 3).reshape(inputs.shape)
    attended_low = attended.astype(jnp.bfloat16)
    mixed = (
        inputs
        + jnp.einsum("sbe,ed->sbd", attended_low, out_weight, preferred_element_type=jnp.float32)
        + bias_rows[2]
    )
    normed, first_pull = jax.vjp(norm_rows, mixed, gain_rows[0], bias_rows[4])
    normed_low = normed.astype(jnp.bfloat16)
    hidden = (
        jnp.einsum("sbd,df->sbf", normed_low, up_weight, preferred_element_type=jnp.float32)
        + up_shift
    )
    active, gelu_pull = jax.vjp(gelu_exact, hidden)
    active_low = active.astype(jnp.bfloat16)
    second = (
        normed
        + jnp.einsum("sbf,fd->sbd", active_low, down_weight, preferred_element_type=jnp.float32)
        + bias_rows[3]
    )
    result, second_pull = jax.vjp(norm_rows, second, gain_rows[1], bias_rows[5])
    kept = (
        inputs_low,
        query,
        keys,
        values,
        log_total,
        attended,
        attended_low,
        normed_low,
        active_low,
        first_pull,
        gelu_pull,
        second_pull,
    )
    return (result, kept)


def backward_layer(upstream, fetched, kept, head_shape):
    qkv_weight, out_weight, up_weight, down_weight = (
        fetched[0],
        fetched[1],
        fetched[2],
        fetched[3],
    )
    (
        inputs_low,
        query,
        keys,
        values,
        log_total,
        attended,
        attended_low,
        normed_low,
        active_low,
        first_pull,
        gelu_pull,
        second_pull,
    ) = kept
    seq_count, block_len, head_count, head_dim = head_shape
    row_axes = (0, 1)
    second_grad, gain_two, shift_two = second_pull(upstream)
    down_in = second_grad.astype(jnp.bfloat16)
    down_grad = jnp.einsum("sbf,sbd->fd", active_low, down_in, preferred_element_type=jnp.float32)
    down_shift = jnp.sum(down_in.astype(jnp.float32), row_axes)
    active_grad = jnp.einsum(
        "sbd,fd->sbf", down_in, down_weight, preferred_element_type=jnp.float32
    )
    hidden_grad = gelu_pull(active_grad)[0].astype(jnp.bfloat16)
    up_grad = jnp.einsum("sbd,sbf->df", normed_low, hidden_grad, preferred_element_type=jnp.float32)
    up_shift_grad = jnp.sum(hidden_grad.astype(jnp.float32), row_axes)
    normed_grad = second_grad + jnp.einsum(
        "sbf,df->sbd", hidden_grad, up_weight, preferred_element_type=jnp.float32
    )
    mixed_grad, gain_one, shift_one = first_pull(normed_grad)
    out_in = mixed_grad.astype(jnp.bfloat16)
    out_weight_grad = jnp.einsum(
        "sbe,sbd->ed", attended_low, out_in, preferred_element_type=jnp.float32
    )
    out_shift = jnp.sum(out_in.astype(jnp.float32), row_axes)
    attend_grad = (
        jnp.einsum("sbd,ed->sbe", out_in, out_weight, preferred_element_type=jnp.float32)
        .astype(jnp.bfloat16)
        .reshape(head_shape)
    )
    delta_rows = jnp.sum(attend_grad.astype(jnp.float32) * attended.reshape(head_shape), -1)
    lse_rows = log_total.transpose(0, 2, 1)
    lse_all, delta_all = (
        lax.all_gather(lse_rows, "blk", axis=1, tiled=True),
        lax.all_gather(delta_rows, "blk", axis=1, tiled=True),
    )
    delta_heads = delta_rows.transpose(0, 2, 1)
    key_part = lax.all_gather(keys, "blk", axis=1, tiled=True)
    value_part = lax.all_gather(values, "blk", axis=1, tiled=True)
    scores = (
        jnp.einsum("sqhd,skhd->shqk", query, key_part, preferred_element_type=jnp.float32)
        * SCORE_SCALE
    )
    probs = jnp.exp(scores - log_total[..., None])
    prob_grad = jnp.einsum(
        "sqhd,skhd->shqk", attend_grad, value_part, preferred_element_type=jnp.float32
    )
    score_grad = (probs * (prob_grad - delta_heads[..., None])).astype(jnp.bfloat16)
    query_grad = (
        jnp.einsum("shqk,skhd->sqhd", score_grad, key_part, preferred_element_type=jnp.float32)
        * SCORE_SCALE
    )
    query_part = lax.all_gather(query, "blk", axis=1, tiled=True)
    grad_part = lax.all_gather(attend_grad, "blk", axis=1, tiled=True)
    lse_part = lse_all.transpose(0, 2, 1)
    delta_part = delta_all.transpose(0, 2, 1)
    scores = (
        jnp.einsum("sqhd,skhd->shqk", query_part, keys, preferred_element_type=jnp.float32)
        * SCORE_SCALE
    )
    probs = jnp.exp(scores - lse_part[..., None])
    value_acc = jnp.einsum(
        "shqk,sqhd->skhd", probs.astype(jnp.bfloat16), grad_part, preferred_element_type=jnp.float32
    )
    prob_grad = jnp.einsum("sqhd,skhd->shqk", grad_part, values, preferred_element_type=jnp.float32)
    score_grad = (probs * (prob_grad - delta_part[..., None])).astype(jnp.bfloat16)
    key_acc = (
        jnp.einsum("shqk,sqhd->skhd", score_grad, query_part, preferred_element_type=jnp.float32)
        * SCORE_SCALE
    )
    flat_shape = (seq_count, block_len, head_count * head_dim)
    query_low = query_grad.reshape(flat_shape).astype(jnp.bfloat16)
    key_low = key_acc.reshape(flat_shape).astype(jnp.bfloat16)
    value_low = value_acc.reshape(flat_shape).astype(jnp.bfloat16)
    proj_grad = jnp.concatenate((query_low, key_low, value_low), -1)
    qkv_grad = jnp.einsum("sbd,sbe->de", inputs_low, proj_grad, preferred_element_type=jnp.float32)
    query_shift = jnp.sum(query_low.astype(jnp.float32), row_axes)
    value_shift = jnp.sum(value_low.astype(jnp.float32), row_axes)
    inputs_grad = mixed_grad + jnp.einsum(
        "sbe,de->sbd", proj_grad, qkv_weight, preferred_element_type=jnp.float32
    )
    shift_rows = jnp.stack((query_shift, value_shift, out_shift, down_shift, shift_one, shift_two))
    gain_grad = jnp.stack((gain_one, gain_two))
    return (
        inputs_grad,
        (qkv_grad, out_weight_grad, up_grad, down_grad, shift_rows, up_shift_grad, gain_grad),
    )


def shards(
    hidden_in,
    mask_index,
    mask_count,
    replacement,
    out_grad,
    w_qkv,
    w_out,
    w_up,
    w_down,
    biases,
    up_bias,
    gains,
):
    seq_count, block_len, model_width = hidden_in.shape
    layer_count = w_qkv.shape[0]
    head_shape = (seq_count, block_len, HEADS, model_width // HEADS)
    offset = lax.axis_index("blk") * block_len
    places = offset + jnp.arange(block_len, dtype=jnp.int32)
    slot_ids = jnp.arange(mask_index.shape[1], dtype=jnp.int32)
    hit_table = (mask_index[:, None, :] == places[None, :, None]) & (
        slot_ids[None, None, :] < mask_count[:, None, None]
    )
    hit_low = hit_table.astype(jnp.bfloat16)
    chosen = jnp.any(hit_table, -1, keepdims=True)
    placed = jnp.einsum("sbm,smd->sbd", hit_low, replacement, preferred_element_type=jnp.float32)
    current = jnp.where(chosen, placed, hidden_in.astype(jnp.float32))
    upstream = jnp.einsum("sbm,smd->sbd", hit_low, out_grad, preferred_element_type=jnp.float32)
    shard_shapes = (w_qkv.shape[1:], w_out.shape[1:], w_up.shape[1:], w_down.shape[1:])
    saved_weights = []
    saved_state = []
    for layer_idx in range(layer_count):
        fetched = (
            lax.all_gather(w_qkv[layer_idx], ("batch", "blk"), axis=0, tiled=True),
            lax.all_gather(w_out[layer_idx], ("batch", "blk"), axis=0, tiled=True),
            lax.all_gather(w_up[layer_idx], ("batch", "blk"), axis=0, tiled=True),
            lax.all_gather(w_down[layer_idx], ("batch", "blk"), axis=0, tiled=True),
            lax.all_gather(biases[layer_idx], ("batch", "blk"), axis=1, tiled=True),
            lax.all_gather(up_bias[layer_idx], ("batch", "blk"), axis=0, tiled=True),
            lax.all_gather(gains[layer_idx], ("batch", "blk"), axis=1, tiled=True),
        )
        saved_weights.append(None)
        current, state = forward_layer(current, fetched, head_shape)
        saved_state.append(state)
    grad_now = upstream
    summed = [None] * layer_count
    for layer_idx in reversed(range(layer_count)):
        fetched = (
            lax.all_gather(w_qkv[layer_idx], ("batch", "blk"), axis=0, tiled=True),
            lax.all_gather(w_out[layer_idx], ("batch", "blk"), axis=0, tiled=True),
            lax.all_gather(w_up[layer_idx], ("batch", "blk"), axis=0, tiled=True),
            lax.all_gather(w_down[layer_idx], ("batch", "blk"), axis=0, tiled=True),
            lax.all_gather(biases[layer_idx], ("batch", "blk"), axis=1, tiled=True),
            lax.all_gather(up_bias[layer_idx], ("batch", "blk"), axis=0, tiled=True),
            lax.all_gather(gains[layer_idx], ("batch", "blk"), axis=1, tiled=True),
        )
        grad_now, terms = backward_layer(grad_now, fetched, saved_state[layer_idx], head_shape)
        flat_terms = (
            terms[0].reshape(-1, 128),
            terms[1].reshape(-1, 128),
            terms[2].reshape(-1, 128),
            terms[3].reshape(-1, 128),
            terms[4],
            terms[5],
            terms[6],
        )
        reduced = (
            lax.psum_scatter(flat_terms[0], ("batch", "blk"), scatter_dimension=0, tiled=True),
            lax.psum_scatter(flat_terms[1], ("batch", "blk"), scatter_dimension=0, tiled=True),
            lax.psum_scatter(flat_terms[2], ("batch", "blk"), scatter_dimension=0, tiled=True),
            lax.psum_scatter(flat_terms[3], ("batch", "blk"), scatter_dimension=0, tiled=True),
            lax.psum_scatter(flat_terms[4], ("batch", "blk"), scatter_dimension=1, tiled=True),
            lax.psum_scatter(flat_terms[5], ("batch", "blk"), scatter_dimension=0, tiled=True),
            lax.psum_scatter(flat_terms[6], ("batch", "blk"), scatter_dimension=1, tiled=True),
        )
        summed[layer_idx] = tuple(
            (reduced[member].reshape(shard_shapes[member]) for member in range(4))
        ) + tuple(reduced[4:])
    stacked = [jnp.stack([entry[member] for entry in summed]) for member in range(7)]
    return (
        current.astype(jnp.bfloat16),
        grad_now,
        stacked[0],
        stacked[1],
        stacked[2],
        stacked[3],
        stacked[4],
        stacked[5],
        stacked[6],
    )


def solution(mesh):
    return jax.shard_map(
        shards,
        mesh=mesh,
        in_specs=(
            P("batch", "blk", None),
            P("batch", None),
            P("batch"),
            P("batch", None, None),
            P("batch", None, None),
            P(None, ("batch", "blk"), None),
            P(None, ("batch", "blk"), None),
            P(None, ("batch", "blk"), None),
            P(None, ("batch", "blk"), None),
            P(None, None, ("batch", "blk")),
            P(None, ("batch", "blk")),
            P(None, None, ("batch", "blk")),
        ),
        out_specs=(
            P("batch", "blk", None),
            P("batch", "blk", None),
            P(None, ("batch", "blk"), None),
            P(None, ("batch", "blk"), None),
            P(None, ("batch", "blk"), None),
            P(None, ("batch", "blk"), None),
            P(None, None, ("batch", "blk")),
            P(None, ("batch", "blk")),
            P(None, None, ("batch", "blk")),
        ),
        check_vma=False,
    )
```

profile of v0, /device:TPU:0, one launch (start us, length us, event | category | flops | bytes accessed | tf_op | source)
XLA Modules:
  0.0 3971.0 jit_solution(496617562575791199)
XLA Ops:
  12.9 70.8 %all-gather.47.cloned.1.call-done = bf16[1,1024,3072]{2,1,0:T(8,128)(2,1)} async-done(((bf16[1,32,3072]{2,1,0:T(8,128)(2,1)}), bf16[1,1024,3072]{2,1,0:T(8,128)(2,1)}) %all-gather.47.cloned.1.call-update) | async-done | bytes 6291472 | tf_op jit(solution)/shard_map/all_gather | solution.py:232
  95.6 96.4 %all-gather.1 = bf16[1,6,1024]{1,0,2:T(2,128)(2,1)S(1)} all-gather(bf16[1,6,32]{1,0,2:T(2,128)(2,1)S(1)} %copy.148), channel_id=3, replica_groups=mesh['batch'=8,'blk'=4] {'batch','blk'}, dimensions={2}, use_global_device_ids=true | all-gather | bytes 12672 | tf_op jit(solution)/shard_map/all_gather | solution.py:236
  192.5 17.3 slice_reduce_fusion.8
  218.6 99.0 %all-gather.3 = bf16[1,2,1024]{1,0,2:T(2,128)(2,1)S(1)} all-gather(bf16[1,2,32]{1,0,2:T(2,128)(2,1)S(1)} %copy.149), channel_id=5, replica_groups=mesh['batch'=8,'blk'=4] {'batch','blk'}, dimensions={2}, use_global_device_ids=true | all-gather | bytes 4224 | tf_op jit(solution)/shard_map/all_gather | solution.py:238
  318.2 63.2 %all-gather.5 = bf16[1,4096]{1,0:T(2,128)(2,1)S(1)} all-gather(bf16[1,128]{1,0:T(2,128)(2,1)S(1)} %get-tuple-element.100), channel_id=7, replica_groups=mesh['batch'=8,'blk'=4] {'batch','blk'}, dimensions={1}, use_global_device_ids=true | all-gather | bytes 8448 | tf_op jit(solution)/shard_map/all_gather | solution.py:237
  388.2 15.8 multiply_reduce_fusion.1
  404.6 15.1 fusion
  419.8 17.2 fusion.146
  442.2 11.5 multiply_convert_fusion.5
  453.7 65.1 %all-gather.53.cloned.1.call-done = bf16[1,4096,1024]{2,1,0:T(8,128)(2,1)} async-done(((bf16[1,128,1024]{2,1,0:T(8,128)(2,1)}), bf16[1,4096,1024]{2,1,0:T(8,128)(2,1)}) %all-gather.53.cloned.1.call-update) | async-done | bytes 8388624 | tf_op jit(solution)/shard_map/all_gather | solution.py:235
  518.9 9.9 fusion.148
  529.1 60.8 %all-gather.55.cloned.1.call-done = bf16[1,1024,3072]{2,1,0:T(8,128)(2,1)} async-done(((bf16[1,32,3072]{2,1,0:T(8,128)(2,1)}), bf16[1,1024,3072]{2,1,0:T(8,128)(2,1)}) %all-gather.55.cloned.1.call-update) | async-done | bytes 6291472 | tf_op jit(solution)/shard_map/all_gather | solution.py:232
  602.1 98.6 %all-gather.8 = bf16[1,6,1024]{1,0,2:T(2,128)(2,1)S(1)} all-gather(bf16[1,6,32]{1,0,2:T(2,128)(2,1)S(1)} %copy.150), channel_id=10, replica_groups=mesh['batch'=8,'blk'=4] {'batch','blk'}, dimensions={2}, use_global_device_ids=true | all-gather | bytes 12672 | tf_op jit(solution)/shard_map/all_gather | solution.py:236
  701.2 17.4 slice_reduce_fusion
  727.1 99.5 %all-gather.10 = bf16[1,2,1024]{1,0,2:T(2,128)(2,1)S(1)} all-gather(bf16[1,2,32]{1,0,2:T(2,128)(2,1)S(1)} %copy.151), channel_id=12, replica_groups=mesh['batch'=8,'blk'=4] {'batch','blk'}, dimensions={2}, use_global_device_ids=true | all-gather | bytes 4224 | tf_op jit(solution)/shard_map/all_gather | solution.py:238
  827.2 63.3 %all-gather.12 = bf16[1,4096]{1,0:T(2,128)(2,1)S(1)} all-gather(bf16[1,128]{1,0:T(2,128)(2,1)S(1)} %get-tuple-element.99), channel_id=14, replica_groups=mesh['batch'=8,'blk'=4] {'batch','blk'}, dimensions={1}, use_global_device_ids=true | all-gather | bytes 8448 | tf_op jit(solution)/shard_map/all_gather | solution.py:237
  899.1 18.8 multiply_reduce_fusion
  917.9 14.8 fusion.2
  932.7 17.3 fusion.149
  955.2 11.5 multiply_convert_fusion.4
  966.7 59.6 %all-gather.61.cloned.1.call-done = bf16[1,4096,1024]{2,1,0:T(8,128)(2,1)} async-done(((bf16[1,128,1024]{2,1,0:T(8,128)(2,1)}), bf16[1,4096,1024]{2,1,0:T(8,128)(2,1)}) %all-gather.61.cloned.1.call-update) | async-done | bytes 8388624 | tf_op jit(solution)/shard_map/all_gather | solution.py:235
  1026.3 9.9 fusion.151
  1040.8 11.7 convert_reduce_fusion
  1052.6 9.3 multiply_reduce_fusion.3
  1072.6 16.5 all_gather.111
  1089.1 19.3 convert_reduce_fusion.5
  1110.6 34.5 all_gather.109
  1145.1 18.3 fusion.152
  1163.4 28.3 all-gather.41.cloned.1.call-done
  1191.8 19.7 multiply_convert_fusion.8
  1213.7 15.0 convert_reduce_fusion.4
  1231.0 8.4 multiply_reduce_fusion.4
  1240.5 14.4 convert_reduce_fusion.1
  1255.0 7.2 multiply_reduce_fusion.5
  1284.0 25.4 all_gather.113
  1309.5 18.4 fusion.153
  1329.9 19.3 convert_reduce_fusion.9
  1354.1 14.9 convert_reduce_fusion.8
  1380.4 10.0 convolution_bitcast_fusion.4
  1390.5 13.8 reshape.298
  1406.9 13.7 all_gather.115
  1420.6 18.5 multiply_convert_fusion.6
  1443.8 8.3 convolution_bitcast_fusion.5
  1452.1 13.9 reshape.297
  1467.2 10.4 convolution_bitcast_fusion
  1477.6 18.0 reshape.304
  1497.2 10.5 convolution_bitcast_fusion.2
  1507.7 18.0 reshape.302
  1527.0 10.4 convolution_bitcast_fusion.1
  1537.4 18.0 reshape.303
  1557.0 10.6 convolution_bitcast_fusion.3
  1567.6 18.0 reshape.301
  1586.6 38.0 all-reduce.2
  1626.7 126.3 %reduce-scatter.39.cloned.1.call-done = f32[32,6]{1,0:T(8,128)} async-done(((f32[1024,6]{1,0:T(8,128)}), f32[32,6]{1,0:T(8,128)}) %reduce-scatter.39.cloned.1.call-update) | async-done | bytes 784
  1753.8 145.6 %reduce-scatter.27.cloned.1.call-done = f32[256,128]{1,0:T(8,128)} async-done(((f32[8192,128]{1,0:T(8,128)}), f32[256,128]{1,0:T(8,128)}) %reduce-scatter.27.cloned.1.call-update) | async-done | bytes 131088 | tf_op jit(solution)/shard_map/reduce_scatter | solution.py:267
  1900.3 8.5 add_add_fusion.8
  1908.8 126.0 %reduce-scatter.37.cloned.1.call-done = f32[32,6]{1,0:T(8,128)} async-done(((f32[1024,6]{1,0:T(8,128)}), f32[32,6]{1,0:T(8,128)}) %reduce-scatter.37.cloned.1.call-update) | async-done | bytes 784
  2036.2 144.8 %reduce-scatter.25.cloned.1.call-done = f32[256,128]{1,0:T(8,128)} async-done(((f32[8192,128]{1,0:T(8,128)}), f32[256,128]{1,0:T(8,128)}) %reduce-scatter.25.cloned.1.call-update) | async-done | bytes 131088 | tf_op jit(solution)/shard_map/reduce_scatter | solution.py:267
  2182.6 158.9 %reduce-scatter.23.cloned.1.call-done = f32[768,128]{1,0:T(8,128)} async-done(((f32[24576,128]{1,0:T(8,128)}), f32[768,128]{1,0:T(8,128)}) %reduce-scatter.23.cloned.1.call-update) | async-done | bytes 393232 | tf_op jit(solution)/shard_map/reduce_scatter | solution.py:266
  2342.6 160.4 %reduce-scatter.21.cloned.1.call-done = f32[768,128]{1,0:T(8,128)} async-done(((f32[24576,128]{1,0:T(8,128)}), f32[768,128]{1,0:T(8,128)}) %reduce-scatter.21.cloned.1.call-update) | async-done | bytes 393232 | tf_op jit(solution)/shard_map/reduce_scatter | solution.py:266
  2505.0 363.6 %reduce-scatter.35.cloned.1.call-done = f32[1024,128]{1,0:T(8,128)} async-done(((f32[32768,128]{1,0:T(8,128)}), f32[1024,128]{1,0:T(8,128)}) %reduce-scatter.35.cloned.1.call-update) | async-done | bytes 524304 | tf_op jit(solution)/shard_map/reduce_scatter | solution.py:269
  2869.7 363.2 %reduce-scatter.31.cloned.1.call-done = f32[1024,128]{1,0:T(8,128)} async-done(((f32[32768,128]{1,0:T(8,128)}), f32[1024,128]{1,0:T(8,128)}) %reduce-scatter.31.cloned.1.call-update) | async-done | bytes 524304 | tf_op jit(solution)/shard_map/reduce_scatter | solution.py:268
  3234.1 363.2 %reduce-scatter.33.cloned.1.call-done = f32[1024,128]{1,0:T(8,128)} async-done(((f32[32768,128]{1,0:T(8,128)}), f32[1024,128]{1,0:T(8,128)}) %reduce-scatter.33.cloned.1.call-update) | async-done | bytes 524304 | tf_op jit(solution)/shard_map/reduce_scatter | solution.py:269
  3599.4 362.3 %reduce-scatter.29.cloned.1.call-done = f32[1024,128]{1,0:T(8,128)} async-done(((f32[32768,128]{1,0:T(8,128)}), f32[1024,128]{1,0:T(8,128)}) %reduce-scatter.29.cloned.1.call-update) | async-done | bytes 524304 | tf_op jit(solution)/shard_map/reduce_scatter | solution.py:268
  (338 shorter events, 168.9 us)
Async XLA Ops:
  7.2 1029.4 %copy-start = (bf16[2,153,1024]{2,0,1:T(2,128)(2,1)S(1)}, bf16[2,153,1024]{2,0,1:T(2,128)(2,1)}, u32[]{:S(2)}) copy-start(bf16[2,153,1024]{2,0,1:T(2,128)(2,1)} %param.16) | copy-start | bytes 1880068
  7.2 76.6 %all-gather.47.cloned.1.call-start = ((), (), s32[]{:S(2)}) async-start(), calls=%async_computation.28 | async-start | bytes 6488064 | tf_op jit(solution)/shard_map/all_gather | solution.py:232
  9.1 379.1 %all-gather.31.cloned.1.call-start = ((), (), s32[]{:S(2)}) async-start(), calls=%async_computation.12 | async-start | bytes 5242880 | tf_op jit(solution)/shard_map/all_gather | solution.py:39
  12.9 76.4 %copy-start.4 = (f32[2,256,1024]{2,1,0:T(8,128)}, f32[2,256,1024]{2,1,0:T(8,128)S(1)}, u32[]{:S(2)}) copy-start(f32[2,256,1024]{2,1,0:T(8,128)S(1)} %convert_select_fusion) | copy-start | bytes 6291460
  95.4 324.4 %all-gather.33.cloned.1.call-start = ((), (), s32[]{:S(2)}) async-start(), calls=%async_computation.13 | async-start | bytes 5242880 | tf_op jit(solution)/shard_map/all_gather | solution.py:40
  209.8 309.1 %copy-start.61 = (f32[1024]{0:T(1024)}, f32[1024]{0:T(1024)S(1)}, u32[]{:S(2)}) copy-start(f32[1024]{0:T(1024)S(1)} %get-tuple-element.60) | copy-start | bytes 12292
  209.8 740.1 %copy-start.29 = (f32[1024]{0:T(1024)}, f32[1024]{0:T(1024)S(1)}, u32[]{:S(2)}) copy-start(f32[1024]{0:T(1024)S(1)} %get-tuple-element.58) | copy-start | bytes 12292
  212.7 5.7 copy-start.66
  212.7 105.4 %copy-start.65 = (bf16[2,128]{1,0:T(2,128)(2,1)S(1)}, bf16[2,128]{1,0:T(2,128)(2,1)}, u32[]{:S(2)}) copy-start(bf16[2,128]{1,0:T(2,128)(2,1)} %param.22) | copy-start | bytes 1540
  214.1 222.9 %all-gather.49.cloned.1.call-start = ((), (), s32[]{:S(2)}) async-start(), calls=%async_computation.29 | async-start | bytes 2162688 | tf_op jit(solution)/shard_map/all_gather | solution.py:233
  214.8 227.4 %all-gather.51.cloned.1.call-start = ((), (), s32[]{:S(2)}) async-start(), calls=%async_computation.30 | async-start | bytes 8650752 | tf_op jit(solution)/shard_map/all_gather | solution.py:234
  215.7 303.1 %all-gather.53.cloned.1.call-start = ((), (), s32[]{:S(2)}) async-start(), calls=%async_computation.31 | async-start | bytes 8650752 | tf_op jit(solution)/shard_map/all_gather | solution.py:235
  217.7 372.3 %all-gather.55.cloned.1.call-start = ((), (), s32[]{:S(2)}) async-start(), calls=%async_computation.32 | async-start | bytes 6488064 | tf_op jit(solution)/shard_map/all_gather | solution.py:232
  218.4 680.6 %all-gather.35.cloned.1.call-start = ((), (), s32[]{:S(2)}) async-start(), calls=%async_computation.14 | async-start | bytes 5242880 | tf_op jit(solution)/shard_map/all_gather | solution.py:39
  381.4 60.8 %copy-start.44 = (f32[1,4096]{1,0:T(1,128)}, f32[1,4096]{1,0:T(1,128)S(1)}, u32[]{:S(2)}) copy-start(f32[1,4096]{1,0:T(1,128)S(1)} %convert_element_type.293) | copy-start | bytes 49156
  387.6 131.2 %copy-start.47 = (f32[1024]{0:T(1024)}, f32[1024]{0:T(1024)S(1)}, u32[]{:S(2)}) copy-start(f32[1024]{0:T(1024)S(1)} %get-tuple-element.57) | copy-start | bytes 12292
  388.2 15.9 copy-start.2
  419.7 17.3 copy-start.31
  419.8 17.3 copy-start.5
  440.4 78.4 %copy-start.34 = (f32[2,256]{1,0:T(2,128)}, f32[2,256]{1,0:T(2,128)S(1)}, u32[]{:S(2)}) copy-start(f32[2,256]{1,0:T(2,128)S(1)} %broadcast_multiply_fusion.3) | copy-start | bytes 6148
  442.1 11.6 copy-start.39
  442.2 76.7 %copy-start.54 = (f32[2,256]{1,0:T(2,128)}, f32[2,256]{1,0:T(2,128)S(1)}, u32[]{:S(2)}) copy-start(f32[2,256]{1,0:T(2,128)S(1)} %fusion.119) | copy-start | bytes 6148
  529.1 66.6 %copy-start.41 = (f32[2,256]{1,0:T(2,128)}, f32[2,256]{1,0:T(2,128)S(1)}, u32[]{:S(2)}) copy-start(f32[2,256]{1,0:T(2,128)S(1)} %multiply_reduce_fusion.14) | copy-start | bytes 6148
  601.9 330.8 %all-gather.37.cloned.1.call-start = ((), (), s32[]{:S(2)}) async-start(), calls=%async_computation.15 | async-start | bytes 5242880 | tf_op jit(solution)/shard_map/all_gather | solution.py:40
  718.6 307.7 %copy-start.63 = (f32[1024]{0:T(1024)}, f32[1024]{0:T(1024)S(1)}, u32[]{:S(2)}) copy-start(f32[1024]{0:T(1024)S(1)} %get-tuple-element.52) | copy-start | bytes 12292
  725.1 224.9 %all-gather.57.cloned.1.call-start = ((), (), s32[]{:S(2)}) async-start(), calls=%async_computation.33 | async-start | bytes 2162688 | tf_op jit(solution)/shard_map/all_gather | solution.py:233
  725.6 229.5 %all-gather.59.cloned.1.call-start = ((), (), s32[]{:S(2)}) async-start(), calls=%async_computation.34 | async-start | bytes 8650752 | tf_op jit(solution)/shard_map/all_gather | solution.py:234
  726.4 299.9 %all-gather.61.cloned.1.call-start = ((), (), s32[]{:S(2)}) async-start(), calls=%async_computation.35 | async-start | bytes 8650752 | tf_op jit(solution)/shard_map/all_gather | solution.py:235
  727.0 418.2 %all-gather.39.cloned.1.call-start = ((), (), s32[]{:S(2)}) async-start(), calls=%async_computation.16 | async-start | bytes 5242880 | tf_op jit(solution)/shard_map/all_gather | solution.py:162
  896.7 165.1 %copy-start.50 = (f32[1024]{0:T(1024)}, f32[1024]{0:T(1024)S(1)}, u32[]{:S(2)}) copy-start(f32[1024]{0:T(1024)S(1)} %get-tuple-element.49) | copy-start | bytes 12292
  899.0 292.8 %all-gather.41.cloned.1.call-start = ((), (), s32[]{:S(2)}) async-start(), calls=%async_computation.17 | async-start | bytes 5242880 | tf_op jit(solution)/shard_map/all_gather | solution.py:163
  953.5 108.4 %copy-start.37 = (f32[2,256]{1,0:T(2,128)}, f32[2,256]{1,0:T(2,128)S(1)}, u32[]{:S(2)}) copy-start(f32[2,256]{1,0:T(2,128)S(1)} %broadcast_multiply_fusion.1) | copy-start | bytes 6148
  955.1 106.7 %copy-start.57 = (f32[2,256]{1,0:T(2,128)}, f32[2,256]{1,0:T(2,128)S(1)}, u32[]{:S(2)}) copy-start(f32[2,256]{1,0:T(2,128)S(1)} %fusion.121) | copy-start | bytes 6148
  1026.3 10.3 copy-start.53
  1040.0 12.6 copy-start.19
  1040.8 11.8 copy-start.11
  1069.6 239.8 %all-gather.43.cloned.1.call-start = ((), (), s32[]{:S(2)}) async-start(), calls=%async_computation.18 | async-start | bytes 5242880 | tf_op jit(solution)/shard_map/all_gather | solution.py:162
  1070.2 283.8 %all-gather.45.cloned.1.call-start = ((), (), s32[]{:S(2)}) async-start(), calls=%async_computation.19 | async-start | bytes 5242880 | tf_op jit(solution)/shard_map/all_gather | solution.py:163
  1231.0 8.4 copy-start.42
  1239.4 15.5 slice-start
  1240.4 14.5 copy-start.21
  1240.4 14.5 copy-start.8
  1240.4 14.5 copy-start.35
  1240.5 14.5 copy-start.48
  1240.5 14.5 copy-start.55
  1240.5 14.5 slice-start.1
  1255.0 7.2 copy-start.40
  1270.0 315.7 %reduce-scatter.43.cloned.1.call-start = ((), (), s32[]{:S(2)}) async-start(), calls=%async_computation.39 | async-start | bytes 540672
  1271.1 354.2 %reduce-scatter.41.cloned.1.call-start = ((), (), s32[]{:S(2)}) async-start(), calls=%async_computation.38 | async-start | bytes 540672
  1272.2 480.7 %reduce-scatter.39.cloned.1.call-start = ((), (), s32[]{:S(2)}) async-start(), calls=%async_computation.37 | async-start | bytes 540672
  1273.5 625.8 %reduce-scatter.27.cloned.1.call-start = ((), (), s32[]{:S(2)}) async-start(), calls=%async_computation.23 | async-start | bytes 4325376 | tf_op jit(solution)/shard_map/reduce_scatter | solution.py:267
  1283.3 751.5 %reduce-scatter.37.cloned.1.call-start = ((), (), s32[]{:S(2)}) async-start(), calls=%async_computation.36 | async-start | bytes 540672
  1309.5 18.4 copy-start.3
  1370.1 810.9 %reduce-scatter.25.cloned.1.call-start = ((), (), s32[]{:S(2)}) async-start(), calls=%async_computation.22 | async-start | bytes 4325376 | tf_op jit(solution)/shard_map/reduce_scatter | solution.py:267
  1379.8 961.7 %reduce-scatter.23.cloned.1.call-start = ((), (), s32[]{:S(2)}) async-start(), calls=%async_computation.21 | async-start | bytes 12976128 | tf_op jit(solution)/shard_map/reduce_scatter | solution.py:266
  1404.3 16.3 copy-start.18
  1404.3 1098.7 %reduce-scatter.21.cloned.1.call-start = ((), (), s32[]{:S(2)}) async-start(), calls=%async_computation.20 | async-start | bytes 12976128 | tf_op jit(solution)/shard_map/reduce_scatter | solution.py:266
  1466.0 1402.6 %reduce-scatter.35.cloned.1.call-start = ((), (), s32[]{:S(2)}) async-start(), calls=%async_computation.27 | async-start | bytes 17301504 | tf_op jit(solution)/shard_map/reduce_scatter | solution.py:269
  1495.6 1737.3 %reduce-scatter.31.cloned.1.call-start = ((), (), s32[]{:S(2)}) async-start(), calls=%async_computation.25 | async-start | bytes 17301504 | tf_op jit(solution)/shard_map/reduce_scatter | solution.py:268
  1525.8 2071.5 %reduce-scatter.33.cloned.1.call-start = ((), (), s32[]{:S(2)}) async-start(), calls=%async_computation.26 | async-start | bytes 17301504 | tf_op jit(solution)/shard_map/reduce_scatter | solution.py:269
  1555.4 2406.3 %reduce-scatter.29.cloned.1.call-start = ((), (), s32[]{:S(2)}) async-start(), calls=%async_computation.24 | async-start | bytes 17301504 | tf_op jit(solution)/shard_map/reduce_scatter | solution.py:268
  1585.6 314.7 %copy-start.14 = (f32[2,256,1024]{2,1,0:T(8,128)S(1)}, f32[2,256,1024]{2,1,0:T(8,128)}, u32[]{:S(2)}) copy-start(f32[2,256,1024]{2,1,0:T(8,128)} %copy-done.13) | copy-start | bytes 6291460
  1585.6 314.7 %copy-start.60 = (f32[2,256]{1,0:T(2,128)S(1)}, f32[2,256]{1,0:T(2,128)}, u32[]{:S(2)}) copy-start(f32[2,256]{1,0:T(2,128)} %copy-done.59) | copy-start | bytes 6148
  2504.1 1459.9 %copy-start.1 = (bf16[2,153,1024]{2,0,1:T(2,128)(2,1)S(1)}, bf16[2,153,1024]{2,0,1:T(2,128)(2,1)}, u32[]{:S(2)}) copy-start(bf16[2,153,1024]{2,0,1:T(2,128)(2,1)} %param.16) | copy-start | bytes 1880068
  (37 other events, 73.3 us)
Sparse Core Ops, SparseCore 0:
  11.5 72.2 all-gather.46
  95.5 86.7 all-gather.30
  214.2 87.7 all-gather.32
  304.8 54.9 all-gather.48
  363.2 76.2 all-gather.50
  442.8 75.9 all-gather.52
  521.7 68.1 all-gather.54
  602.0 86.8 all-gather.34
  725.2 84.3 all-gather.36
  812.3 55.2 all-gather.56
  871.1 76.2 all-gather.58
  950.2 76.0 all-gather.60
  1027.8 81.2 all-gather.38
  1110.5 81.2 all-gather.40
  1193.2 76.9 all-gather.42
  1271.6 82.4 all-gather.44
  1356.2 130.8 reduce-scatter.42
  1489.2 130.4 reduce-scatter.40
  1622.5 130.4 reduce-scatter.38
  1755.2 144.1 reduce-scatter.26
  1901.7 133.0 reduce-scatter.36
  2037.1 143.8 reduce-scatter.24
  2187.0 154.4 reduce-scatter.22
  2348.4 154.5 reduce-scatter.20
  2505.3 363.2 reduce-scatter.34
  2870.8 362.1 reduce-scatter.30
  3235.1 362.1 reduce-scatter.32
  3599.6 362.1 reduce-scatter.28
where the time goes:
time: 3980 us; the launch traced here: 3970 us
  waiting for transfers between devices  2610 us (66%)
  blocking collectives  648 us (16%)
  matrix products  411 us (10%)
  local copies, waits for them, and re-layouts  231 us (6%)
  other arithmetic  56.3 us (1%)
    reduce_scatter x2, waiting for transfers between devices, shards(): lax.psum_scatter(flat_terms[3], ('batch', 'blk'), scatter_dimension=0, ti...  727 us
    reduce_scatter x2, waiting for transfers between devices, shards(): lax.psum_scatter(flat_terms[2], ('batch', 'blk'), scatter_dimension=0, ti...  726 us
    reduce_scatter x2, waiting for transfers between devices, shards(): lax.psum_scatter(flat_terms[0], ('batch', 'blk'), scatter_dimension=0, ti...  319 us
    reduce_scatter x2, waiting for transfers between devices, shards(): lax.psum_scatter(flat_terms[1], ('batch', 'blk'), scatter_dimension=0, ti...  290 us
    unnamed x32, waiting for transfers between devices  256 us
    all_gather x2, blocking collectives, shards(): lax.all_gather(gains[layer_idx], ('batch', 'blk'), axis=1, tiled=True)  199 us
    all_gather x2, blocking collectives, shards(): lax.all_gather(biases[layer_idx], ('batch', 'blk'), axis=1, tiled=True)  195 us
    all_gather x2, waiting for transfers between devices, shards(): lax.all_gather(w_qkv[layer_idx], ('batch', 'blk'), axis=0, tiled=True)  132 us
  transfers between devices with their start and end apart: 28, of which 16 were waited for; matrix products, arithmetic and copies ran while one was open for 16% of the time, Pallas kernels for 0%

commit v1 on v0

--- a/solution.py
+++ b/solution.py
@@ -1,11 +1,16 @@
+import functools
+
 import jax
 import jax.numpy as jnp
 from jax import lax
+from jax.experimental import pallas as pl
+from jax.experimental.pallas import tpu as pltpu
 from jax.sharding import PartitionSpec as P
 
 HEADS = 16
 
 
+BOTH = ("batch", "blk")
 NORM_EPS = 1e-12
 SCORE_SCALE = 0.125
 
@@ -196,7 +201,7 @@
     )
 
 
-def shards(
+def general_shards(
     hidden_in,
     mask_index,
     mask_count,
@@ -229,13 +234,13 @@
     saved_state = []
     for layer_idx in range(layer_count):
         fetched = (
-            lax.all_gather(w_qkv[layer_idx], ("batch", "blk"), axis=0, tiled=True),
-            lax.all_gather(w_out[layer_idx], ("batch", "blk"), axis=0, tiled=True),
-            lax.all_gather(w_up[layer_idx], ("batch", "blk"), axis=0, tiled=True),
-            lax.all_gather(w_down[layer_idx], ("batch", "blk"), axis=0, tiled=True),
-            lax.all_gather(biases[layer_idx], ("batch", "blk"), axis=1, tiled=True),
-            lax.all_gather(up_bias[layer_idx], ("batch", "blk"), axis=0, tiled=True),
-            lax.all_gather(gains[layer_idx], ("batch", "blk"), axis=1, tiled=True),
+            lax.all_gather(w_qkv[layer_idx], BOTH, axis=0, tiled=True),
+            lax.all_gather(w_out[layer_idx], BOTH, axis=0, tiled=True),
+            lax.all_gather(w_up[layer_idx], BOTH, axis=0, tiled=True),
+            lax.all_gather(w_down[layer_idx], BOTH, axis=0, tiled=True),
+            lax.all_gather(biases[layer_idx], BOTH, axis=1, tiled=True),
+            lax.all_gather(up_bias[layer_idx], BOTH, axis=0, tiled=True),
+            lax.all_gather(gains[layer_idx], BOTH, axis=1, tiled=True),
         )
         saved_weights.append(None)
         current, state = forward_layer(current, fetched, head_shape)
@@ -244,13 +249,13 @@
     summed = [None] * layer_count
     for layer_idx in reversed(range(layer_count)):
         fetched = (
-            lax.all_gather(w_qkv[layer_idx], ("batch", "blk"), axis=0, tiled=True),
-            lax.all_gather(w_out[layer_idx], ("batch", "blk"), axis=0, tiled=True),
-            lax.all_gather(w_up[layer_idx], ("batch", "blk"), axis=0, tiled=True),
-            lax.all_gather(w_down[layer_idx], ("batch", "blk"), axis=0, tiled=True),
-            lax.all_gather(biases[layer_idx], ("batch", "blk"), axis=1, tiled=True),
-            lax.all_gather(up_bias[layer_idx], ("batch", "blk"), axis=0, tiled=True),
-            lax.all_gather(gains[layer_idx], ("batch", "blk"), axis=1, tiled=True),
+            lax.all_gather(w_qkv[layer_idx], BOTH, axis=0, tiled=True),
+            lax.all_gather(w_out[layer_idx], BOTH, axis=0, tiled=True),
+            lax.all_gather(w_up[layer_idx], BOTH, axis=0, tiled=True),
+            lax.all_gather(w_down[layer_idx], BOTH, axis=0, tiled=True),
+            lax.all_gather(biases[layer_idx], BOTH, axis=1, tiled=True),
+            lax.all_gather(up_bias[layer_idx], BOTH, axis=0, tiled=True),
+            lax.all_gather(gains[layer_idx], BOTH, axis=1, tiled=True),
         )
         grad_now, terms = backward_layer(grad_now, fetched, saved_state[layer_idx], head_shape)
         flat_terms = (
@@ -263,13 +268,13 @@
             terms[6],
         )
         reduced = (
-            lax.psum_scatter(flat_terms[0], ("batch", "blk"), scatter_dimension=0, tiled=True),
-            lax.psum_scatter(flat_terms[1], ("batch", "blk"), scatter_dimension=0, tiled=True),
-            lax.psum_scatter(flat_terms[2], ("batch", "blk"), scatter_dimension=0, tiled=True),
-            lax.psum_scatter(flat_terms[3], ("batch", "blk"), scatter_dimension=0, tiled=True),
-            lax.psum_scatter(flat_terms[4], ("batch", "blk"), scatter_dimension=1, tiled=True),
-            lax.psum_scatter(flat_terms[5], ("batch", "blk"), scatter_dimension=0, tiled=True),
-            lax.psum_scatter(flat_terms[6], ("batch", "blk"), scatter_dimension=1, tiled=True),
+            lax.psum_scatter(flat_terms[0], BOTH, scatter_dimension=0, tiled=True),
+            lax.psum_scatter(flat_terms[1], BOTH, scatter_dimension=0, tiled=True),
+            lax.psum_scatter(flat_terms[2], BOTH, scatter_dimension=0, tiled=True),
+            lax.psum_scatter(flat_terms[3], BOTH, scatter_dimension=0, tiled=True),
+            lax.psum_scatter(flat_terms[4], BOTH, scatter_dimension=1, tiled=True),
+            lax.psum_scatter(flat_terms[5], BOTH, scatter_dimension=0, tiled=True),
+            lax.psum_scatter(flat_terms[6], BOTH, scatter_dimension=1, tiled=True),
         )
         summed[layer_idx] = tuple(
             (reduced[member].reshape(shard_shapes[member]) for member in range(4))
@@ -288,34 +293,1241 @@
     )
 
 
+NT = (((1,), (1,)), ((), ()))
+TN = (((0,), (0,)), ((), ()))
+F32 = jnp.float32
+BF = jnp.bfloat16
+
+
+def dot(a, b, dims):
+    return lax.dot_general(a, b, dims, preferred_element_type=F32)
+
+
+MESH = pl.DeviceIdType.MESH
+UNITS = 12
+TILE = 256
+LAGS = (3, 2, 4, 5)
+DIRECT = 8
+
+
+def place_of():
+    batch = lax.axis_index("batch")
+    return batch, lax.axis_index("blk"), batch // 4, lax.rem(batch // 2, 2), lax.rem(batch, 2)
+
+
+def columns(tile):
+    return pl.ds(pl.multiple_of(tile * TILE, TILE), TILE)
+
+
+def forward_kernel(
+    first_ref,
+    qkv_in,
+    out_in,
+    up_in,
+    down_in,
+    small_ref,
+    w_ref,
+    out_ref,
+    rows_ref,
+    lse_ref,
+    low_ref,
+    qkv_ref,
+    kv_ref,
+    mix_ref,
+    nrm_ref,
+    act_ref,
+    slope_ref,
+    unit_ref,
+    scale_ref,
+    cur,
+    low,
+    qkv,
+    sib,
+    mix,
+    nrm,
+    acc,
+    act,
+    slope,
+    unit,
+    scale,
+    wbuf,
+    shard,
+    small_all,
+    local_sems,
+    own_sems,
+    save_sems,
+    send_sems,
+    recv_sems,
+    side_send,
+    side_recv,
+    turn_send,
+    turn_recv,
+    layers,
+):
+    batch, z, y, x, core = place_of()
+    total = layers * UNITS
+    yx = 2 * y + x
+    column = 4 * y + 2 * x
+    here = {"x": (batch ^ 2, z), "y": (batch ^ 4, z), "core": (batch ^ 1, z)}
+
+    def remote(src, dst, send, recv, device):
+        return pltpu.make_async_remote_copy(
+            src_ref=src,
+            dst_ref=dst,
+            send_sem=send,
+            recv_sem=recv,
+            device_id=device,
+            device_id_type=MESH,
+        )
+
+    flying = {}
+
+    def launch(kind, unit_id, copies):
+        flying[kind, unit_id] = copies
+        for copy in copies:
+            copy.start()
+
+    def landed(kind, unit_id):
+        for copy in flying[kind, unit_id]:
+            copy.wait_recv()
+
+    def hop(unit_id, slot, src, dst, device):
+        return remote(src, dst, send_sems.at[unit_id, slot], recv_sems.at[unit_id, slot], device)
+
+    own_rows = pl.ds(pl.multiple_of(z * 32, 32), 32)
+
+    def straight(unit_id):
+        return 1024 if unit_id < DIRECT else 1024 - 128
+
+    def along(unit_id):
+        cols = pl.ds(0, straight(unit_id))
+        dst = w_ref.at[unit_id, yx, core, own_rows, cols]
+        src = shard.at[unit_id, :, cols]
+        copies = []
+        if unit_id >= DIRECT:
+            edge = pl.ds(1024 - 128, 128)
+            piece, spot = shard.at[unit_id, :, edge], w_ref.at[unit_id, yx, core, own_rows, edge]
+            copies += [hop(unit_id, 8, piece, spot, here["x"]), hop(unit_id, 9, piece, spot, here["y"])]
+        for step in (1, 2, 3):
+            copies.append(hop(unit_id, step - 1, src, dst, (batch, lax.rem(z + step, 4))))
+        return copies
+
+    def across(unit_id):
+        line = w_ref.at[unit_id, yx, core, :, pl.ds(0, straight(unit_id))]
+        copies = []
+        if unit_id >= DIRECT:
+            edge = pl.ds(1024 - 128, 128)
+            if unit_id % 2:
+                piece, to = w_ref.at[unit_id, 2 * y + 1 - x, core, own_rows, edge], here["y"]
+            else:
+                piece, to = w_ref.at[unit_id, 2 - 2 * y + x, core, own_rows, edge], here["x"]
+            copies.append(hop(unit_id, 10, piece, piece, to))
+        copies += [hop(unit_id, 3, line, line, here["x"]), hop(unit_id, 4, line, line, here["y"])]
+        return copies
+
+    def corner(unit_id):
+        full = straight(unit_id)
+        half = 384 if full < 1024 and unit_id % 2 else 512
+        left = w_ref.at[unit_id, 2 * y + 1 - x, core, :, pl.ds(0, half)]
+        right = w_ref.at[unit_id, 2 - 2 * y + x, core, :, pl.ds(half, full - half)]
+        copies = []
+        if unit_id >= DIRECT:
+            block = w_ref.at[unit_id, :, core, own_rows, pl.ds(1024 - 128, 128)]
+            for step in (1, 2, 3):
+                to = (batch, lax.rem(z + step, 4))
+                copies.append(hop(unit_id, 10 + step, block, block, to))
+        copies += [hop(unit_id, 5, left, left, here["y"]), hop(unit_id, 6, right, right, here["x"])]
+        return copies
+
+    def inner(unit_id):
+        block = w_ref.at[unit_id, :, core]
+        return [hop(unit_id, 7, block, block, here["core"])]
+
+    def side(slot, src, dst, device):
+        return remote(src, dst, side_send.at[slot], side_recv.at[slot], device)
+
+    def layout(layer):
+        base = layer * UNITS
+        for part in range(3):
+            shard[base + part] = qkv_in[layer, :, part * 1024 : part * 1024 + 1024]
+        shard[base + 3] = out_in[layer]
+        lane = lax.broadcasted_iota(jnp.int32, (32, 128), 1) // 32
+        for j in range(4):
+            shard[base + 5 + 2 * j] = down_in[layer, j * 32 : j * 32 + 32]
+            for block in range(8):
+                made = None
+                for part in range(4):
+                    start = (4 * block + part) * 128
+                    value = up_in[layer, :, start : start + 128].astype(F32)
+                    if part != j:
+                        value = pltpu.roll(value, ((part - j) * 32) % 128, 1)
+                    made = value if made is None else jnp.where(lane == part, value, made)
+                shard[base + 4 + 2 * j, :, block * 128 : block * 128 + 128] = made.astype(BF)
+
+    owns = [
+        pltpu.make_async_copy(
+            shard.at[unit_id], w_ref.at[unit_id, yx, core, own_rows], own_sems.at[unit_id]
+        )
+        for unit_id in range(total)
+    ]
+    mine = small_all.at[y, x, core, z]
+    mine[...] = small_ref[...]
+    launch(
+        "small",
+        0,
+        [side(step - 1, small_ref, mine, (batch, lax.rem(z + step, 4))) for step in (1, 2, 3)],
+    )
+
+    def turn(j, half):
+        to = 2 * core + j
+        block = lax.rem(to - z + 4, 4)
+        src = first_ref.at[j, pl.ds(half * 128, 128)]
+        dst = low.at[pl.ds(pl.multiple_of(block * 128, 128), 128)]
+        send, recv = turn_send.at[2 * j + half], turn_recv.at[block]
+        return (
+            lambda: pltpu.make_async_copy(src, dst, local_sems.at[0]),
+            lambda: remote(src, dst, send, recv, (column + half, to)),
+            jnp.logical_and(to == z, core == half),
+        )
+
+    def turned(block):
+        spot = low.at[pl.ds(block * 128, 128)]
+        return remote(spot, spot, turn_send.at[0], turn_recv.at[block], here["core"])
+
+    for layer in range(layers):
+        layout(layer)
+        if layer == 0:
+            for unit_id in range(2):
+                owns[unit_id].start()
+                launch("along", unit_id, along(unit_id))
+            for j in range(2):
+                for half in range(2):
+                    local, away, stays = turn(j, half)
+                    pl.when(stays)(lambda: local().start())
+                    pl.when(jnp.logical_not(stays))(lambda: away().start())
+            for unit_id in range(2, LAGS[0]):
+                owns[unit_id].start()
+                launch("along", unit_id, along(unit_id))
+    own_turn = core == z // 2
+
+    def small_hop(number):
+        landed("small", number - 1)
+        if number == 1:
+            line = small_all.at[y, x, core]
+            launch("small", 1, [side(3, line, line, here["x"])])
+        elif number == 2:
+            plane = small_all.at[y, :, core]
+            launch("small", 2, [side(4, plane, plane, here["y"])])
+        elif number == 3:
+            cube = small_all.at[:, :, core]
+            launch("small", 3, [side(5, cube, cube, here["core"])])
+
+    def begin():
+        small_hop(4)
+        for block in range(8):
+            four = small_all[block // 4, (block // 2) % 2, block % 2]
+            rows_ref[:, block * 128 : block * 128 + 128] = (four[0] + four[1]) + (four[2] + four[3])
+        local = turn(0, 0)[0]
+        pl.when(own_turn)(lambda: local().wait())
+        pl.when(jnp.logical_not(own_turn))(lambda: turned(0).wait_recv())
+        for block in range(1, 4):
+            turned(block).wait_recv()
+
+        def body(step, carry):
+            rows = pl.ds(pl.multiple_of(step * 64, 64), 64)
+            cur[rows] = low[rows].astype(F32)
+            return carry
+
+        lax.fori_loop(0, 8, body, 0)
+
+    saves = {}
+
+    def save(name, src, dst, slot):
+        if name in saves:
+            saves[name].wait()
+        saves[name] = pltpu.make_async_copy(src, dst, save_sems.at[slot])
+        saves[name].start()
+
+    def settle(*names):
+        for name in names:
+            if name in saves:
+                saves.pop(name).wait()
+
+    def weight(tile):
+        return wbuf[:, :, :, columns(tile)].reshape(1024, TILE)
+
+    def norm(layer, which, gain_row, shift_row):
+        gain = rows_ref[pl.ds(gain_row, 1)]
+        shift_by = rows_ref[pl.ds(shift_row, 1)]
+
+        def body(step, carry):
+            rows = pl.ds(step * 64, 64)
+            value = acc[rows]
+            center = value - jnp.mean(value, -1, keepdims=True)
+            spread = jnp.mean(center * center, -1, keepdims=True)
+            root = lax.rsqrt(spread + NORM_EPS)
+            normal = center * root
+            unit[which, rows] = normal
+            scale[which, rows] = jnp.broadcast_to(root, (64, 128))
+            result = normal * gain + shift_by
+            if which == 0:
+                acc[rows] = result + rows_ref[pl.ds(layer * 12 + 3, 1)]
+                nrm[rows] = result.astype(BF)
+            else:
+                cur[rows] = result
+                low[rows] = result.astype(BF)
+            return carry
+
+        lax.fori_loop(0, 8, body, 0)
+        save(("unit", which), unit.at[which], unit_ref.at[layer, which], 8 + which)
+        save(("scale", which), scale.at[which], scale_ref.at[layer, which], 10 + which)
+
+    def heads(layer, begin, end):
+        def body(j, carry):
+            lanes = pl.ds(pl.multiple_of(j * 128, 128), 128)
+            k_lanes = pl.ds(pl.multiple_of(1024 + j * 128, 128), 128)
+            v_lanes = pl.ds(pl.multiple_of(2048 + j * 128, 128), 128)
+            q = qkv[:, lanes]
+            lane = lax.broadcasted_iota(jnp.int32, q.shape, 1)
+            outs = []
+            for head in range(2):
+                qh = jnp.where((lane // 64) == head, q, jnp.zeros_like(q))
+                s_own = dot(qkv[:, k_lanes], qh, NT)
+                s_sib = dot(sib[layer, 0, :, lanes], qh, NT)
+                top = jnp.maximum(
+                    jnp.max(s_own, 0, keepdims=True), jnp.max(s_sib, 0, keepdims=True)
+                )
+                p_own = jnp.exp(s_own - top)
+                p_sib = jnp.exp(s_sib - top)
+                mass = jnp.sum(p_own, 0, keepdims=True) + jnp.sum(p_sib, 0, keepdims=True)
+                lse_ref[layer, j, pl.ds(head, 1)] = top + jnp.log(mass)
+                o = dot(qkv[:, v_lanes], p_own.astype(BF), TN) + dot(
+                    sib[layer, 1, :, lanes], p_sib.astype(BF), TN
+                )
+                outs.append(o[head * 64 : head * 64 + 64] / mass)
+            mix[:, lanes] = jnp.transpose(jnp.concatenate(outs, 0)).astype(BF)
+            return carry
+
+        lax.fori_loop(begin, end, body, 0)
+
+    def compute(unit_id):
+        layer, kind = unit_id // UNITS, unit_id % UNITS
+        base = layer * 12
+        fetch = pltpu.make_async_copy(w_ref.at[unit_id], wbuf, local_sems.at[3])
+        fetch.start()
+        if kind == 0:
+            save("low", low, low_ref.at[layer], 0)
+        if kind == 3:
+            heads(layer, 4, 8)
+            save("mix", mix, mix_ref.at[layer], 3)
+        fetch.wait()
+        if kind < 3:
+            bias = rows_ref[pl.ds(base + (0 if kind == 0 else 1), 1)]
+            if kind == 0:
+                settle("qkv")
+            for copy in flying.pop(("kv", (layer - 1, kind)), ()):
+                copy.wait_send()
+
+            def body(tile, carry):
+                value = jnp.dot(low[...], weight(tile), preferred_element_type=F32)
+                cols = columns(tile)
+                if kind != 1:
+                    value = value + rows_ref[pl.ds(base + kind // 2, 1), cols]
+                value = value.astype(BF)
+                if kind == 0:
+                    value = (value.astype(F32) * SCORE_SCALE).astype(BF)
+                qkv[:, columns(tile + 4 * kind)] = value
+                return carry
+
+            lax.fori_loop(0, 4, body, 0)
+            if kind:
+                launch(
+                    "kv",
+                    (layer, kind),
+                    [
+                        side(
+                            6 + 2 * layer + kind - 1,
+                            qkv.at[:, pl.ds(1024 * kind, 1024)],
+                            sib.at[layer, kind - 1],
+                            here["core"],
+                        )
+                    ],
+                )
+            if kind == 2:
+                save("qkv", qkv, qkv_ref.at[layer], 1)
+                landed("kv", (layer, 1))
+                landed("kv", (layer, 2))
+                save("kv", sib.at[layer], kv_ref.at[layer], 2)
+                settle("mix")
+                heads(layer, 0, 4)
+        elif kind == 3:
+            settle("nrm", ("unit", 0), ("scale", 0))
+
+            def body(tile, carry):
+                cols = columns(tile)
+                value = jnp.dot(mix[...], weight(tile), preferred_element_type=F32)
+                acc[:, cols] = cur[:, cols] + value + rows_ref[pl.ds(base + 2, 1), cols]
+                return carry
+
+            lax.fori_loop(0, 4, body, 0)
+            norm(layer, 0, base + 6, base + 4)
+            save("nrm", nrm, nrm_ref.at[layer], 4)
+        elif kind % 2 == 0:
+            j = kind // 2 - 2
+            settle(("act", j), ("slope", j))
+
+            def body(tile, carry):
+                cols = columns(tile)
+                value = jnp.dot(nrm[...], weight(tile), preferred_element_type=F32)
+                value = value + rows_ref[pl.ds(base + 8 + j, 1), cols]
+                gate = 0.5 * (1.0 + lax.erf(value * 0.7071067811865476))
+                act[j, :, cols] = (value * gate).astype(BF)
+                bell = jnp.exp(-0.5 * value * value)
+                slope[j, :, cols] = (gate + value * (0.3989422804014327 * bell)).astype(BF)
+                return carry
+
+            lax.fori_loop(0, 4, body, 0)
+            save(("act", j), act.at[j], act_ref.at[layer, j], 12 + j)
+            save(("slope", j), slope.at[j], slope_ref.at[layer, j], 16 + j)
+        else:
+            j = kind // 2 - 2
+
+            def body(tile, carry):
+                cols = columns(tile)
+                acc[:, cols] += jnp.dot(act[j], weight(tile), preferred_element_type=F32)
+                return carry
+
+            lax.fori_loop(0, 4, body, 0)
+            if j == 3:
+                settle("low", ("unit", 1), ("scale", 1))
+                norm(layer, 1, base + 7, base + 5)
+                if layer == layers - 1:
+                    save("low", low, out_ref, 0)
+
+    ahead, corner_lag, inner_lag, use_lag = LAGS
+    for step in range(total + use_lag):
+        if step + ahead < total:
+            owns[step + ahead].start()
+            launch("along", step + ahead, along(step + ahead))
+        if step < total:
+            owns[step].wait()
+            landed("along", step)
+            launch("across", step, across(step))
+        if 0 < step < 4:
+            small_hop(step)
+        if 0 <= step - corner_lag < total:
+            landed("across", step - corner_lag)
+            launch("corner", step - corner_lag, corner(step - corner_lag))
+        if 0 <= step - inner_lag < total:
+            landed("corner", step - inner_lag)
+            launch("inner", step - inner_lag, inner(step - inner_lag))
+        if step == use_lag:
+            begin()
+        if 0 <= step - use_lag < total:
+            landed("inner", step - use_lag)
+            compute(step - use_lag)
+    for j in range(2):
+        for half in range(2):
+            local, away, stays = turn(j, half)
+            pl.when(jnp.logical_not(stays))(lambda: away().wait_send())
+    for copies in flying.values():
+        for copy in copies:
+            copy.wait_send()
+    settle(*list(saves))
+
+
+def forward_pass(first, w_qkv, w_out, w_up, w_down, small):
+    layers = w_qkv.shape[0]
+    width = first.shape[2]
+    rows = first.shape[0] * first.shape[1]
+    any_spec = pl.BlockSpec(memory_space=pl.ANY)
+    vmem = pl.BlockSpec(memory_space=pltpu.VMEM)
+    shape = jax.ShapeDtypeStruct
+    total = layers * UNITS
+    return pl.pallas_call(
+        functools.partial(forward_kernel, layers=layers),
+        in_specs=[vmem] * 6,
+        out_specs=[any_spec, any_spec, vmem, vmem] + [any_spec] * 9,
+        out_shape=[
+            shape((total, 4, 2, 128, width), BF),
+            shape((rows, width), BF),
+            shape((layers * 12, width), F32),
+            shape((layers, 8, 2, rows), F32),
+            shape((layers, rows, width), BF),
+            shape((layers, rows, 3 * width), BF),
+            shape((layers, 2, rows, width), BF),
+            shape((layers, rows, width), BF),
+            shape((layers, rows, width), BF),
+            shape((layers, 4, rows, width), BF),
+            shape((layers, 4, rows, width), BF),
+            shape((layers, 2, rows, width), F32),
+            shape((layers, 2, rows, 128), F32),
+        ],
+        scratch_shapes=[
+            pltpu.VMEM((rows, width), F32),
+            pltpu.VMEM((rows, width), BF),
+            pltpu.VMEM((rows, 3 * width), BF),
+            pltpu.VMEM((layers, 2, rows, width), BF),
+            pltpu.VMEM((rows, width), BF),
+            pltpu.VMEM((rows, width), BF),
+            pltpu.VMEM((rows, width), F32),
+            pltpu.VMEM((4, rows, width), BF),
+            pltpu.VMEM((4, rows, width), BF),
+            pltpu.VMEM((2, rows, width), F32),
+            pltpu.VMEM((2, rows, 128), F32),
+            pltpu.VMEM((4, 2, 128, width), BF),
+            pltpu.VMEM((total, 32, width), BF),
+            pltpu.VMEM((2, 2, 2, 4, layers * 12, 128), F32),
+            pltpu.SemaphoreType.DMA((4,)),
+            pltpu.SemaphoreType.DMA((total,)),
+            pltpu.SemaphoreType.DMA((20,)),
+            pltpu.SemaphoreType.DMA((total, 14)),
+            pltpu.SemaphoreType.DMA((total, 14)),
+            pltpu.SemaphoreType.DMA((6 + 2 * layers,)),
+            pltpu.SemaphoreType.DMA((6 + 2 * layers,)),
+            pltpu.SemaphoreType.DMA((4,)),
+            pltpu.SemaphoreType.DMA((4,)),
+        ],
+        compiler_params=pltpu.CompilerParams(
+            has_side_effects=True, vmem_limit_bytes=60 << 20
+        ),
+        name="forward_pass",
+    )(first, w_qkv, w_out, w_up, w_down, small)
+
+
+def backward_kernel(
+    top_ref,
+    last_ref,
+    w_ref,
+    rows_ref,
+    lse_ref,
+    low_ref,
+    qkv_ref,
+    kv_ref,
+    mix_ref,
+    nrm_ref,
+    act_ref,
+    slope_ref,
+    unit_ref,
+    scale_ref,
+    last_out,
+    grad_out,
+    qkv_out,
+    out_out,
+    up_out,
+    down_out,
+    bias_out,
+    up_bias_out,
+    gain_out,
+    grad,
+    edge,
+    unit,
+    scale,
+    arena,
+    span,
+    feat,
+    turned,
+    wbuf,
+    send,
+    mine,
+    land,
+    wide,
+    slim,
+    ends,
+    small_all,
+    small_in,
+    staged,
+    up_all,
+    load_sems,
+    store_sems,
+    send_sems,
+    recv_sems,
+    side_send,
+    side_recv,
+    turn_send,
+    turn_recv,
+    layers,
+):
+    batch, z, y, x, core = place_of()
+    total = layers * UNITS
+    here = {"x": (batch ^ 2, z), "y": (batch ^ 4, z), "core": (batch ^ 1, z)}
+    slots = 6
+
+    def remote(src, dst, send_sem, recv_sem, device):
+        return pltpu.make_async_remote_copy(
+            src_ref=src,
+            dst_ref=dst,
+            send_sem=send_sem,
+            recv_sem=recv_sem,
+            device_id=device,
+            device_id_type=MESH,
+        )
+
+    incoming, outgoing = {}, {}
+
+    def launch(kind, number, copies):
+        incoming[kind, number] = copies
+        outgoing[kind, number] = copies
+        for copy in copies:
+            copy.start()
+
+    def landed(kind, number):
+        for copy in incoming.pop((kind, number)):
+            copy.wait_recv()
+
+    def sent(kind, number):
+        for copy in outgoing.pop((kind, number), ()):
+            copy.wait_send()
+
+    def hop(number, slot, src, dst, device):
+        return remote(src, dst, send_sems.at[number, slot], recv_sems.at[number, slot], device)
+
+    def side(slot, src, dst, device):
+        return remote(src, dst, side_send.at[slot], side_recv.at[slot], device)
+
+    loads = {}
+
+    def fetch(name, src, dst, slot):
+        loads[name] = pltpu.make_async_copy(src, dst, load_sems.at[slot])
+        loads[name].start()
+
+    def ready(name):
+        loads.pop(name).wait()
+
+    order = []
+    for layer in reversed(range(layers)):
+        for j in range(4):
+            order += [layer * UNITS + 5 + 2 * j, layer * UNITS + 4 + 2 * j]
+        order += [layer * UNITS + 3, layer * UNITS, layer * UNITS + 1, layer * UNITS + 2]
+
+    def fetch_weight(number):
+        if number < total:
+            fetch(("w", number), w_ref.at[order[number]], wbuf.at[number % 2], number % 2)
+
+    def rows_of(number, tile):
+        return wbuf[number % 2, tile].reshape(TILE, 1024)
+
+    def turn(slot, source):
+        def body(block, carry):
+            rows = pl.ds(pl.multiple_of(block * 128, 128), 128)
+            for half, which in enumerate((core, 1 - core)):
+                lanes = pl.ds(pl.multiple_of(block * 256 + which * 128, 128), 128)
+                turned[slot, half, rows] = jnp.transpose(source[:, lanes])
+            return carry
+
+        lax.fori_loop(0, 4, body, 0)
+
+    def produce(number, slot, upper):
+        buffer = number % 2
+        sent("core", number - 2)
+
+        def body(tile, carry):
+            cols = columns(tile)
+            value = jnp.dot(turned[slot, 1], upper[:, cols], preferred_element_type=F32)
+            send[buffer, :, :, cols] = value.astype(BF).reshape(4, 128, TILE)
+            return carry
+
+        lax.fori_loop(0, 4, body, 0)
+        launch("core", number, [hop(number, 0, send.at[buffer], land.at[number % UNITS], here["core"])])
+
+        def own(tile, carry):
+            cols = columns(tile)
+            value = jnp.dot(turned[slot, 0], upper[:, cols], preferred_element_type=F32)
+            mine[number % slots, :, :, cols] = value.astype(BF).reshape(4, 128, TILE)
+            return carry
+
+        lax.fori_loop(0, 4, own, 0)
+
+    left, right = pl.ds(0, 512), pl.ds(512, 512)
+
+    def stage_core(number):
+        part = land.at[number % UNITS]
+        landed("core", number)
+
+        def body(block, carry):
+            part[block] = (part[block].astype(F32) + mine[number % slots, block].astype(F32)).astype(BF)
+            return carry
+
+        lax.fori_loop(0, 4, body, 0)
+        spot = number % slots
+        launch(
+            "wide",
+            number,
+            [
+                hop(number, 1, part.at[pl.ds(2 - 2 * y, 2), :, left], wide.at[spot, 0], here["y"]),
+                hop(number, 2, part.at[pl.ds(1 - x, 1), :, right], wide.at[spot, 1, pl.ds(0, 1)], here["x"]),
+                hop(number, 3, part.at[pl.ds(3 - x, 1), :, right], wide.at[spot, 1, pl.ds(1, 1)], here["x"]),
+            ],
+        )
+
+    def stage_wide(number):
+        part, spot = land.at[number % UNITS], number % slots
+        landed("wide", number)
+        for block in range(2):
+            spot_y = 2 * y + block
+            value = part[spot_y, :, left].astype(F32) + wide[spot, 0, block].astype(F32)
+            part[spot_y, :, left] = value.astype(BF)
+            spot_x = 2 * block + x
+            value = part[spot_x, :, right].astype(F32) + wide[spot, 1, block].astype(F32)
+            part[spot_x, :, right] = value.astype(BF)
+        launch(
+            "slim",
+            number,
+            [
+                hop(number, 4, part.at[2 * y + 1 - x, :, left], slim.at[spot, 0], here["x"]),
+                hop(number, 5, part.at[2 - 2 * y + x, :, right], slim.at[spot, 1], here["y"]),
+            ],
+        )
+
+    def stage_slim(number):
+        part, spot = land.at[number % UNITS, 2 * y + x], number % slots
+        landed("slim", number)
+        part[:, left] = (part[:, left].astype(F32) + slim[spot, 0].astype(F32)).astype(BF)
+        part[:, right] = (part[:, right].astype(F32) + slim[spot, 1].astype(F32)).astype(BF)
+        copies = []
+        for step in (1, 2, 3):
+            to = lax.rem(z + step, 4)
+            src = part.at[pl.ds(pl.multiple_of(to * 32, 32), 32)]
+            copies.append(hop(number, 5 + step, src, ends.at[spot, step - 1], (batch, to)))
+        launch("ends", number, copies)
+
+    def stage_ends(number):
+        part, spot = land.at[number % UNITS, 2 * y + x], number % slots
+        landed("ends", number)
+        value = part[pl.ds(pl.multiple_of(z * 32, 32), 32)].astype(F32)
+        for step in range(3):
+            value = value + ends[spot, step].astype(F32)
+        layer, kind = order[number] // UNITS, order[number] % UNITS
+        j = kind // 2 - 2
+        if kind > 3 and kind % 2 == 0:
+            lane = lax.broadcasted_iota(jnp.int32, (32, 128), 1) // 32
+            if j == 0 and 4 in stores:
+                stores.pop(4).wait()
+            for block in range(32):
+                spot = pl.ds(block * 128, 128)
+                piece = value[:, block // 4 * 128 : block // 4 * 128 + 128]
+                if j != block % 4:
+                    piece = pltpu.roll(piece, ((j - block % 4) * 32) % 128, 1)
+                up_all[:, spot] = piece if j == 0 else jnp.where(lane == j, piece, up_all[:, spot])
+            if j == 3:
+                stores[4] = pltpu.make_async_copy(up_all, up_out.at[layer], store_sems.at[4])
+                stores[4].start()
+        else:
+            slot = number % 4
+            if slot in stores:
+                stores.pop(slot).wait()
+            staged[slot] = value
+            if kind < 3:
+                dst = qkv_out.at[layer, :, pl.ds(1024 * kind, 1024)]
+            else:
+                dst = out_out.at[layer] if kind == 3 else down_out.at[layer, j]
+            stores[slot] = pltpu.make_async_copy(staged.at[slot], dst, store_sems.at[slot])
+            stores[slot].start()
+        for kind in ("wide", "slim", "ends"):
+            sent(kind, number)
+
+    ticks = [0]
+    stores = {}
+    wide_lag, slim_lag, ends_lag = BACK_LAGS
+
+    def tick():
+        step = ticks[0]
+        ticks[0] += 1
+        if step < total:
+            stage_core(step)
+        if 0 <= step - wide_lag < total:
+            stage_wide(step - wide_lag)
+        if 0 <= step - slim_lag < total:
+            stage_slim(step - slim_lag)
+        if 0 <= step - ends_lag < total:
+            stage_ends(step - ends_lag)
+
+    def norm(base, gain_row, shift_row, sum_row):
+        gain = rows_ref[pl.ds(base + gain_row, 1)]
+
+        def body(step, carry):
+            gains, shifts, sums = carry
+            rows = pl.ds(step * 64, 64)
+            value = grad[rows]
+            normal = unit[rows]
+            scaled = value * gain
+            inner = jnp.mean(scaled * normal, -1, keepdims=True)
+            centre = jnp.mean(scaled, -1, keepdims=True)
+            result = scale[rows][:, :1] * (scaled - centre - normal * inner)
+            grad[rows] = result
+            rounded = result.astype(BF)
+            edge[rows] = rounded
+            return (
+                gains + jnp.sum(value * normal, 0, keepdims=True),
+                shifts + jnp.sum(value, 0, keepdims=True),
+                sums + jnp.sum(rounded.astype(F32), 0, keepdims=True),
+            )
+
+        zero = jnp.zeros((1, 1024), F32)
+        gains, shifts, sums = lax.fori_loop(0, 8, body, (zero, zero, zero))
+        put_row(base + gain_row, gains)
+        put_row(base + shift_row, shifts)
+        put_row(base + sum_row, sums)
+
+    def put_row(row, value):
+        for block in range(8):
+            small_all[block // 2, block % 2, row : row + 1] = value[:, block * 128 : block * 128 + 128]
+
+    def heads(layer, begin, end):
+        def body(j, carry):
+            lanes = pl.ds(pl.multiple_of(j * 128, 128), 128)
+            q = arena[0, :, lanes]
+            do = span[:, lanes]
+            lane = lax.broadcasted_iota(jnp.int32, q.shape, 1)
+            prod = jnp.transpose(do.astype(F32) * feat[1, :, lanes].astype(F32))
+            dq = []
+            sums = [[None, None], [None, None]]
+            for head in range(2):
+                pick = (lane // 64) == head
+                qh = jnp.where(pick, q, jnp.zeros_like(q))
+                dh = jnp.where(pick, do, jnp.zeros_like(do))
+                delta = jnp.sum(prod[head * 64 : head * 64 + 64], 0, keepdims=True)
+                lse = lse_ref[layer, j, pl.ds(head, 1)]
+                dqh = None
+                for half in range(2):
+                    k = arena[1 + 2 * half, :, lanes]
+                    v = arena[2 + 2 * half, :, lanes]
+                    p = jnp.exp(dot(k, qh, NT) - lse)
+                    ds = (p * (dot(v, dh, NT) - delta)).astype(BF)
+                    dv = jnp.dot(p.astype(BF), dh, preferred_element_type=F32)
+                    dk = jnp.dot(ds, qh, preferred_element_type=F32)
+                    part = dot(ds, k, TN)
+                    dqh = part if dqh is None else dqh + part
+                    sums[half][0] = dk if head == 0 else sums[half][0] + dk
+                    sums[half][1] = dv if head == 0 else sums[half][1] + dv
+                dq.append(dqh)
+            arena[5, :, lanes] = (jnp.where(lane < 64, dq[0], dq[1]) * SCORE_SCALE).astype(BF)
+            arena[6, :, lanes] = sums[0][0].astype(BF)
+            arena[7, :, lanes] = sums[0][1].astype(BF)
+            arena[8, :, lanes] = sums[1][0].astype(BF)
+            arena[9, :, lanes] = sums[1][1].astype(BF)
+            return carry
+
+        lax.fori_loop(begin, end, body, 0)
+
+    def row_sum(row, slot):
+        def body(step, carry):
+            rows = pl.ds(pl.multiple_of(step * 64, 64), 64)
+            return carry + jnp.sum(arena[slot, rows].astype(F32), 0, keepdims=True)
+
+        put_row(row, lax.fori_loop(0, 8, body, jnp.zeros((1, 1024), F32)))
+
+    def pull(number, upper):
+        def body(tile, carry):
+            cols = columns(tile)
+            grad[:, cols] += dot(upper[...], rows_of(number, tile), NT)
+            return carry
+
+        ready(("w", number))
+        lax.fori_loop(0, 4, body, 0)
+        fetch_weight(number + 2)
+
+    def load_attention(layer):
+        for part in range(3):
+            fetch(("qkv", part), qkv_ref.at[layer, :, pl.ds(1024 * part, 1024)], arena.at[part], 2 + part)
+        for part in range(2):
+            fetch(("kv", part), kv_ref.at[layer, part], arena.at[3 + part], 5 + part)
+
+    column = 4 * y + 2 * x
+    seat = 2 * lax.rem(z, 2) + core
+    stays = core == z // 2
+
+    def homeward(which, block, src, dst):
+        rows = src.at[pl.ds(block * 128, 128)]
+        spot = dst.at[lax.rem(z, 2), pl.ds(pl.multiple_of(core * 128, 128), 128)]
+        to = (column + z // 2, lax.rem(z - block + 4, 4))
+        return (
+            lambda: pltpu.make_async_copy(rows, spot, load_sems.at[14 + which]),
+            lambda: remote(rows, spot, turn_send.at[which, block], turn_recv.at[which, seat], to),
+        )
+
+    def turn_start(which, src, dst):
+        for block in range(4):
+            local, away = homeward(which, block, src, dst)
+            if block:
+                away().start()
+            else:
+                pl.when(stays)(lambda: local().start())
+                pl.when(jnp.logical_not(stays))(lambda: away().start())
+
+    def turn_end(which, src, dst):
+        for block in range(4):
+            local, away = homeward(which, block, src, dst)
+            if block:
+                away().wait_send()
+            else:
+                pl.when(stays)(lambda: local().wait())
+                pl.when(jnp.logical_not(stays))(lambda: away().wait_send())
+        for place in range(4):
+            spot = dst.at[place // 2, pl.ds(place % 2 * 128, 128)]
+            came = remote(spot, spot, turn_send.at[which, 0], turn_recv.at[which, place], here["core"])
+            own = jnp.logical_and(2 * core + place // 2 == z, core == place % 2)
+            pl.when(jnp.logical_not(own))(came.wait_recv)
+
+    fetch("top", top_ref, grad, 7)
+    turn_start(0, last_ref, last_out)
+    first = True
+    for layer in reversed(range(layers)):
+        base = layer * 12
+        start = (layers - 1 - layer) * UNITS
+        if first:
+            fetch("unit", unit_ref.at[layer, 1], unit, 8)
+            fetch("scale", scale_ref.at[layer, 1], scale, 9)
+            fetch_weight(0)
+            fetch_weight(1)
+            load_attention(layer)
+            ready("top")
+        fetch("act", act_ref.at[layer, 0], arena.at[8], 10)
+        fetch("slope", slope_ref.at[layer, 0], arena.at[9], 11)
+        fetch("nrm", nrm_ref.at[layer], feat.at[0], 12)
+        fetch("mix", mix_ref.at[layer], feat.at[1], 13)
+        first = False
+        ready("unit")
+        ready("scale")
+        norm(base, 7, 5, 3)
+        fetch("unit", unit_ref.at[layer, 0], unit, 8)
+        fetch("scale", scale_ref.at[layer, 0], scale, 9)
+        ready("nrm")
+        turn(0, feat.at[0])
+        fetch("low", low_ref.at[layer], feat.at[0], 12)
+        for j in range(4):
+            number = start + 2 * j
+            ready("act")
+            turn(1, arena.at[8])
+            if j < 3:
+                fetch("act", act_ref.at[layer, j + 1], arena.at[8], 10)
+            produce(number, 1, edge)
+            ready(("w", number))
+            ready("slope")
+
+            def body(tile, carry):
+                cols = columns(tile)
+                value = dot(edge[...], rows_of(number, tile), NT)
+                value = (arena[9, :, cols].astype(F32) * value).astype(BF)
+                span[:, cols] = value
+                total_row = jnp.sum(value.astype(F32), 0, keepdims=True)
+                for block in range(2):
+                    small_all[tile, block, pl.ds(base + 8 + j, 1)] = total_row[
+                        :, block * 128 : block * 128 + 128
+                    ]
+                return carry
+
+            lax.fori_loop(0, 4, body, 0)
+            fetch_weight(number + 2)
+            if j < 3:
+                fetch("slope", slope_ref.at[layer, j + 1], arena.at[9], 11)
+            produce(number + 1, 0, span)
+            pull(number + 1, span)
+            tick()
+        ready("unit")
+        ready("scale")
+        norm(base, 6, 4, 2)
+        if layer:
+            fetch("unit", unit_ref.at[layer - 1, 1], unit, 8)
+            fetch("scale", scale_ref.at[layer - 1, 1], scale, 9)
+        ready("mix")
+        turn(1, feat.at[1])
+        number = start + 8
+        ready(("w", number))
+
+        def body(tile, carry):
+            span[:, columns(tile)] = dot(edge[...], rows_of(number, tile), NT).astype(BF)
+            return carry
+
+        lax.fori_loop(0, 4, body, 0)
+        fetch_weight(number + 2)
+        tick()
+        produce(number, 1, edge)
+        for part in range(3):
+            ready(("qkv", part))
+        for part in range(2):
+            ready(("kv", part))
+        for group in range(4):
+            heads(layer, 2 * group, 2 * group + 2)
+            tick()
+        place = layers - 1 - layer
+        for part in range(2):
+            launch(
+                "keys",
+                2 * place + part,
+                [side(2 * place + part, arena.at[8 + part], arena.at[10 + part], here["core"])],
+            )
+        if layer:
+            load_attention(layer - 1)
+        ready("low")
+        turn(0, feat.at[0])
+        for part in range(3):
+            number = start + 9 + part
+            if part:
+                landed("keys", 2 * place + part - 1)
+
+                def body(step, carry):
+                    rows = pl.ds(pl.multiple_of(step * 64, 64), 64)
+                    value = arena[5 + part, rows].astype(F32) + arena[9 + part, rows].astype(F32)
+                    arena[5 + part, rows] = value.astype(BF)
+                    return carry
+
+                lax.fori_loop(0, 8, body, 0)
+            if part != 1:
+                row_sum(base + part // 2, 5 + part)
+            produce(number, 0, arena.at[5 + part])
+            pull(number, arena.at[5 + part])
+            if part < 2:
+                tick()
+        sent("keys", 2 * place)
+        sent("keys", 2 * place + 1)
+        if layer == 0:
+
+            def body(step, carry):
+                rows = pl.ds(pl.multiple_of(step * 64, 64), 64)
+                edge[rows] = grad[rows].astype(BF)
+                return carry
+
+            lax.fori_loop(0, 8, body, 0)
+            turn_start(1, edge, grad_out)
+        tick()
+    base = 2 * layers
+
+    def small_core():
+        launch("small", 0, [side(base, small_all.at[:, 1 - core], small_in.at[pl.ds(0, 4)], here["core"])])
+
+    def small_y():
+        landed("small", 0)
+        sent("small", 0)
+        small_all[:, core] = small_all[:, core] + small_in[0:4]
+        launch(
+            "small",
+            1,
+            [side(base + 1, small_all.at[pl.ds(2 - 2 * y, 2), core], small_in.at[pl.ds(4, 2)], here["y"])],
+        )
+
+    def small_x():
+        landed("small", 1)
+        sent("small", 1)
+        for block in range(2):
+            small_all[2 * y + block, core] = small_all[2 * y + block, core] + small_in[4 + block]
+        launch(
+            "small",
+            2,
+            [side(base + 2, small_all.at[2 * y + 1 - x, core], small_in.at[6], here["x"])],
+        )
+
+    def small_z():
+        landed("small", 2)
+        sent("small", 2)
+        own = small_all.at[2 * y + x, core]
+        own[...] = own[...] + small_in[6]
+        launch(
+            "small",
+            3,
+            [
+                side(base + 2 + step, own, small_in.at[6 + step], (batch, lax.rem(z + step, 4)))
+                for step in (1, 2, 3)
+            ],
+        )
+
+    def small_end():
+        landed("small", 3)
+        sent("small", 3)
+        value = small_all[2 * y + x, core]
+        for step in (1, 2, 3):
+            value = value + small_in[6 + step]
+        mine_row = value[:, 0:32]
+        for place in range(1, 4):
+            mine_row = jnp.where(z == place, value[:, place * 32 : place * 32 + 32], mine_row)
+        for layer in range(layers):
+            top = layer * 12
+            bias_out[layer] = mine_row[top : top + 6]
+            gain_out[layer] = mine_row[top + 6 : top + 8]
+            for j in range(4):
+                up_bias_out[layer : layer + 1, j * 32 : j * 32 + 32] = mine_row[top + 8 + j : top + 9 + j]
+
+    queue = [small_core, small_y, small_x, small_z, small_end]
+    while ticks[0] < total + ends_lag or queue:
+        if queue:
+            queue.pop(0)()
+        if ticks[0] < total + ends_lag:
+            tick()
+    for kind, number in list(outgoing):
+        sent(kind, number)
+    for copy in stores.values():
+        copy.wait()
+    turn_end(0, last_ref, last_out)
+    turn_end(1, edge, grad_out)
+
+
+BACK_LAGS = (2, 4, 5)
+
+
+def backward_pass(top, last, saved):
+    w, rows, lse, low, qkv, kv, mix, nrm, act, slope, unit, scale = saved
+    total = w.shape[0]
+    layers = total // UNITS
+    tokens, width = top.shape
+    any_spec = pl.BlockSpec(memory_space=pl.ANY)
+    vmem = pl.BlockSpec(memory_space=pltpu.VMEM)
+    shape = jax.ShapeDtypeStruct
+    return pl.pallas_call(
+        functools.partial(backward_kernel, layers=layers),
+        in_specs=[any_spec] * 3 + [vmem, vmem] + [any_spec] * 9,
+        out_specs=[any_spec] * 6 + [vmem] * 3,
+        out_shape=[
+            shape((2, tokens // 2, width), BF),
+            shape((2, tokens // 2, width), BF),
+            shape((layers, 32, 3 * width), F32),
+            shape((layers, 32, width), F32),
+            shape((layers, 32, 4 * width), F32),
+            shape((layers, 4, 32, width), F32),
+            shape((layers, 6, 32), F32),
+            shape((layers, 128), F32),
+            shape((layers, 2, 32), F32),
+        ],
+        scratch_shapes=[
+            pltpu.VMEM((tokens, width), F32),
+            pltpu.VMEM((tokens, width), BF),
+            pltpu.VMEM((tokens, width), F32),
+            pltpu.VMEM((tokens, 128), F32),
+            pltpu.VMEM((12, tokens, width), BF),
+            pltpu.VMEM((tokens, width), BF),
+            pltpu.VMEM((2, tokens, width), BF),
+            pltpu.VMEM((2, 2, width // 2, tokens), BF),
+            pltpu.VMEM((2, 4, 2, 128, width), BF),
+            pltpu.VMEM((2, 4, 128, width), BF),
+            pltpu.VMEM((6, 4, 128, width), BF),
+            pltpu.VMEM((UNITS, 4, 128, width), BF),
+            pltpu.VMEM((6, 2, 2, 128, width // 2), BF),
+            pltpu.VMEM((6, 2, 128, width // 2), BF),
+            pltpu.VMEM((6, 3, 32, width), BF),
+            pltpu.VMEM((4, 2, layers * 12, 128), F32),
+            pltpu.VMEM((10, layers * 12, 128), F32),
+            pltpu.VMEM((4, 32, width), F32),
+            pltpu.VMEM((32, 4 * width), F32),
+            pltpu.SemaphoreType.DMA((16,)),
+            pltpu.SemaphoreType.DMA((5,)),
+            pltpu.SemaphoreType.DMA((total, 9)),
+            pltpu.SemaphoreType.DMA((total, 9)),
+            pltpu.SemaphoreType.DMA((2 * layers + 6,)),
+            pltpu.SemaphoreType.DMA((2 * layers + 6,)),
+            pltpu.SemaphoreType.DMA((2, 4)),
+            pltpu.SemaphoreType.DMA((2, 4)),
+        ],
+        compiler_params=pltpu.CompilerParams(has_side_effects=True, vmem_limit_bytes=60 << 20),
+        name="backward_pass",
+    )(top, last, w, rows, lse, low, qkv, kv, mix, nrm, act, slope, unit, scale)
+
+
+def swap(value, bit):
+    return lax.ppermute(value, "batch", [(place, place ^ bit) for place in range(8)])
+
+
+def take(value, index, axis):
+    return lax.dynamic_index_in_dim(value, index, axis, keepdims=False)
+
+
+def small_rows(biases, up_bias, gains):
+    layers = biases.shape[0]
+    rows = jnp.concatenate((biases, gains, up_bias.reshape(layers, 4, 32)), 1).astype(F32)
+    wide = jnp.tile(rows.reshape(layers * 12, 32), (1, 4))
+    lane = lax.broadcasted_iota(jnp.int32, wide.shape, 1)
+    return jnp.where(lane // 32 == lax.axis_index("blk"), wide, 0.0)
+
+
+def column_shards(
+    hidden_in,
+    mask_index,
+    mask_count,
+    replacement,
+    out_grad,
+    w_qkv,
+    w_out,
+    w_up,
+    w_down,
+    biases,
+    up_bias,
+    gains,
+):
+    batch = lax.axis_index("batch")
+    z = lax.axis_index("blk")
+    core = lax.rem(batch, 2)
+    seq_count, block_len, width = hidden_in.shape
+    layers = w_qkv.shape[0]
+    slots = mask_index.shape[1]
+    per = width // 32
+
+    slot_ids = jnp.arange(slots, dtype=jnp.int32)
+    used = slot_ids[None, :] < mask_count[:, None]
+    slot_place = jnp.where(used, mask_index, -1)
+    places = z * block_len + jnp.arange(block_len, dtype=jnp.int32)
+    hits = slot_place[:, None, :] == places[None, :, None]
+    placed = jnp.einsum("sbm,smd->sbd", hits.astype(BF), replacement, preferred_element_type=F32)
+    first = jnp.where(jnp.any(hits, -1, keepdims=True), placed.astype(BF), hidden_in)
+
+    mine = lax.rem(z, 2)
+    came_grad = swap(take(out_grad, mine, 0), 1)
+    came_place = swap(take(slot_place, mine, 0).astype(F32), 1)
+    here = (z // 2) == core
+    top_grad = jnp.where(here, take(out_grad, mine, 0), came_grad)
+    top_place = jnp.where(here, take(slot_place, mine, 0), came_place.astype(jnp.int32))
+    blocks = lax.rem(z - jnp.arange(4, dtype=jnp.int32) + 4, 4)
+    token_place = (
+        blocks[:, None] * block_len
+        + core * (block_len // 2)
+        + jnp.arange(block_len // 2, dtype=jnp.int32)[None, :]
+    ).reshape(-1)
+    top_hits = (token_place[:, None] == top_place[None, :]).astype(BF)
+    upstream = jnp.dot(top_hits, top_grad, preferred_element_type=F32)
+
+    results = forward_pass(first, w_qkv, w_out, w_up, w_down, small_rows(biases, up_bias, gains))
+    last, grad, qkv, out, up, down, bias_rows, up_rows, gain_rows = backward_pass(
+        upstream, results[1], (results[0],) + tuple(results[2:])
+    )
+    return (
+        last,
+        grad.astype(F32),
+        qkv,
+        out,
+        up,
+        down.reshape(layers, 4 * per, width),
+        bias_rows,
+        up_rows,
+        gain_rows,
+    )
+
+
 def solution(mesh):
+    fits = mesh.shape["batch"] == 8 and mesh.shape["blk"] == 4
     return jax.shard_map(
-        shards,
+        column_shards if fits else general_shards,
         mesh=mesh,
         in_specs=(
-            P("batch", "blk", None),
+            P(*BOTH, None),
             P("batch", None),
             P("batch"),
             P("batch", None, None),
             P("batch", None, None),
-            P(None, ("batch", "blk"), None),
-            P(None, ("batch", "blk"), None),
-            P(None, ("batch", "blk"), None),
-            P(None, ("batch", "blk"), None),
-            P(None, None, ("batch", "blk")),
-            P(None, ("batch", "blk")),
-            P(None, None, ("batch", "blk")),
+            P(None, BOTH, None),
+            P(None, BOTH, None),
+            P(None, BOTH, None),
+            P(None, BOTH, None),
+            P(None, None, BOTH),
+            P(None, BOTH),
+            P(None, None, BOTH),
         ),
         out_specs=(
-            P("batch", "blk", None),
-            P("batch", "blk", None),
-            P(None, ("batch", "blk"), None),
-            P(None, ("batch", "blk"), None),
-            P(None, ("batch", "blk"), None),
-            P(None, ("batch", "blk"), None),
-            P(None, None, ("batch", "blk")),
-            P(None, ("batch", "blk")),
-            P(None, None, ("batch", "blk")),
+            P(*BOTH, None),
+            P(*BOTH, None),
+            P(None, BOTH, None),
+            P(None, BOTH, None),
+            P(None, BOTH, None),
+            P(None, BOTH, None),
+            P(None, None, BOTH),
+            P(None, BOTH),
+            P(None, None, BOTH),
         ),
         check_vma=False,
     )

time: 3980 us -> 571 us (0.14)
  waiting for transfers between devices: 2610 us -> 0.01 us
  blocking collectives: 648 us -> 0 us
  Pallas kernels: 0 us -> 549 us
  matrix products: 411 us -> 3.44 us
  local copies, waits for them, and re-layouts: 231 us -> 9.11 us
  other arithmetic: 56.3 us -> 4.58 us
    reduce_scatter x8 -> x0, waiting for transfers between devices: 2060 us -> none  [the longest x2 727 us: shards(): lax.psum_scatter(flat_terms[3], ('batch', 'blk'), scatter_dimension=0, ti...]
    all_gather x10 -> x0, blocking collectives: 610 us -> none  [the longest x2 199 us: shards(): lax.all_gather(gains[layer_idx], ('batch', 'blk'), axis=1, tiled=True)]
    pallas_call x0 -> x2, Pallas kernels: none -> 549 us  [the longest x1 279 us: backward_pass(): pl.pallas_call(functools.partial(backward_kernel, layers=layers), in_spec...]
    dot_general x38 -> x2, matrix products: 411 us -> 3.44 us  [the longest x1 1.8 us: column_shards(): upstream = jnp.dot(top_hits, top_grad, preferred_element_type=F32)]
    all_gather x16 -> x0, waiting for transfers between devices: 290 us -> none  [the longest x2 132 us: shards(): lax.all_gather(w_qkv[layer_idx], ('batch', 'blk'), axis=0, tiled=True)]
    unnamed x32 -> x0, waiting for transfers between devices: 256 us -> none
    reshape x8 -> x2, local copies, waits for them, and re-layouts: 110 us -> 0.09 us  [small_rows(): up_bias.reshape(layers, 4, 32)]
    slice x15 -> x0, local copies, waits for them, and re-layouts: 59.1 us -> none  [the longest x4 47.1 us: forward_layer(): result, second_pull = jax.vjp(norm_rows, second, gain_rows[1], bias_rows[5])]
  transfers between devices with their start and end apart: 28 -> 2, of which waited for: 16 -> 0; matrix products, arithmetic and copies ran while one was open for 16% -> 1% of each run, Pallas kernels for 0% -> 48%
where the time goes in v1:
time: 571 us; the launch traced here: 567 us
  Pallas kernels  549 us (96%)
  local copies, waits for them, and re-layouts  9.11 us (2%)
    pallas_call x1, Pallas kernels, backward_pass(): pl.pallas_call(functools.partial(backward_kernel, layers=layers), in_spec...  279 us
    pallas_call x1, Pallas kernels, forward_pass(): pl.pallas_call(functools.partial(forward_kernel, layers=layers), in_specs...  270 us
  transfers between devices with their start and end apart: 2, of which 0 were waited for; matrix products, arithmetic and copies ran while one was open for 1% of the time, Pallas kernels for 48%

profile of v1, /device:TPU:0, one launch (start us, length us, event | category | flops | bytes accessed | tf_op | source)
XLA Modules:
  0.0 567.5 jit_solution(7837987727389531988)
XLA Ops:
  0.6 0.0 copy-start
  0.7 0.0 copy-start.9
  0.7 0.0 copy-start.11
  0.7 0.0 copy-start.7
  0.7 0.0 copy-start.12
  0.7 0.9 compare_select_fusion
  1.6 0.5 collective-permute-start
  2.1 1.7 constant_dynamic-slice_fusion
  3.8 0.1 copy.35
  3.9 0.1 collective-permute-start.1
  4.1 0.0 copy-done.9
  4.1 0.1 compare_reduce_fusion
  4.3 0.0 copy-done.11
  4.3 0.1 reshape.71
  4.4 0.0 copy-done.7
  4.4 0.1 tile.9
  4.5 0.0 copy-done
  4.5 0.0 copy-done.12
  4.5 1.6 fusion.first_ref
  6.2 0.6 fusion.11.small_ref
  6.8 0.1 add_bitcast_fusion
  6.9 270.0 %forward_pass.1 = (bf16[24,4,2,128,1024]{4,3,2,1,0:T(8,128)(2,1)}, bf16[512,1024]{1,0:T(8,128)(2,1)}, f32[24,1024]{1,0:T(8,128)}, f32[2,8,2,512]{3,2,1,0:T(2,128...) custom-call(bf16[2,256,1024]{2,1,0:T(8,128)(2,1)} %fusion.first_ref,, ...), custom_call_target="tpu_custom_call" | custom-call | tf_op jit(solution)/shard_map/forward_pass/pallas_call | solution.py:747
  276.8 0.0 collective-permute-done
  276.9 0.0 collective-permute-done.1
  276.9 1.8 fusion.2.top_ref
  278.7 278.6 %backward_pass.1 = (bf16[2,256,1024]{2,1,0:T(8,128)(2,1)}, bf16[2,256,1024]{2,1,0:T(8,128)(2,1)}, f32[2,32,3072]{2,1,0:T(8,128)}, f32[2,32,1024]{2,1,0:T(8,128)}...) custom-call(f32[512,1024]{1,0:T(8,128)} %fusion.2.top_ref, ...), custom_call_target="tpu_custom_call" | custom-call | tf_op jit(solution)/shard_map/backward_pass/pallas_call | solution.py:1375
  557.3 0.0 copy-start.4
  557.3 1.4 copy.30
  558.7 0.0 copy-start.5
  558.7 2.9 convert_element_type.29
  561.5 0.0 copy-done.4
  561.5 0.0 copy-start.6
  561.6 0.0 copy-start.3
  561.6 1.0 copy.43
  562.5 0.0 copy-done.5
  562.5 0.0 copy-start.2
  562.5 0.9 copy.44
  563.4 0.0 copy-done.6
  563.4 0.0 copy-start.1
  563.4 0.7 copy.45
  564.1 0.0 copy-done.3
  564.1 0.0 copy-start.10
  564.1 0.0 copy-start.8
  564.1 1.0 copy.46
  565.1 0.0 copy-done.2
  565.1 1.0 copy.47
  566.1 0.0 copy-done.10
  566.1 0.6 copy.48
  566.6 0.0 copy-done.8
  566.6 0.6 copy.49
  567.2 0.0 copy-done.1
  (13 shorter events, 0.1 us)
Async XLA Ops:
  0.6 3.9 copy-start
  0.7 3.5 copy-start.9
  0.7 3.6 copy-start.11
  0.7 3.7 copy-start.7
  0.7 3.8 copy-start.12
  1.6 275.2 %collective-permute-start = (f32[153]{0:T(256)S(1)}, f32[153]{0:T(256)S(1)}, u32[]{:S(2)}, u32[]{:S(2)}) collective-permute-start(f32[153]{0:T(256)S(1)} %convert_element_type.24), channel_id=1, source_target_pairs={{0,4},{4,0},{8,12},{12,8},{16,20},{20,16},{24,28},{28,24},{1,5},{5... | collective-permute-start | bytes 1844 | tf_op jit(solution)/shard_map/ppermute | solution.py:1425
  3.9 272.9 %collective-permute-start.1 = (bf16[153,1024]{1,0:T(8,128)(2,1)S(1)}, bf16[153,1024]{1,0:T(8,128)(2,1)S(1)}, u32[]{:S(2)}, u32[]{:S(2)}) collective-permute-start(bf16[153,1024]{1,0:T(8,128)(2,1)S(1)} %bitcast.7), channel_id=1, source_target_pairs={{0,4},{4,0},{8,12},{12,8},{16,20},{20,16},{24,28},{28,24},{1,5},{5... | collective-permute-start | bytes 940040 | tf_op jit(solution)/shard_map/ppermute | solution.py:1425
  557.3 4.3 copy-start.4
  558.7 3.8 copy-start.5
  561.5 1.9 copy-start.6
  561.6 2.6 copy-start.3
  562.5 2.6 copy-start.2
  563.4 3.8 copy-start.1
  564.1 1.9 copy-start.10
  564.1 2.5 copy-start.8

commit v2 on v1

--- a/solution.py
+++ b/solution.py
@@ -306,8 +306,11 @@
 MESH = pl.DeviceIdType.MESH
 UNITS = 12
 TILE = 256
-LAGS = (3, 2, 4, 5)
+LAGS = (3, 1, 3, 4)
 DIRECT = 8
+TURN_STEPS = (0, 2, 4, 6)
+BEGIN = 9
+BUDGET = 4.5
 
 
 def place_of():
@@ -330,12 +333,10 @@
     out_ref,
     rows_ref,
     lse_ref,
-    low_ref,
     qkv_ref,
     kv_ref,
     mix_ref,
-    nrm_ref,
-    act_ref,
+    flip_ref,
     slope_ref,
     unit_ref,
     scale_ref,
@@ -351,6 +352,7 @@
     unit,
     scale,
     wbuf,
+    flipped,
     shard,
     small_all,
     local_sems,
@@ -497,18 +499,19 @@
     for layer in range(layers):
         layout(layer)
         if layer == 0:
-            for unit_id in range(2):
+            for unit_id in range(1):
                 owns[unit_id].start()
                 launch("along", unit_id, along(unit_id))
-            for j in range(2):
-                for half in range(2):
-                    local, away, stays = turn(j, half)
-                    pl.when(stays)(lambda: local().start())
-                    pl.when(jnp.logical_not(stays))(lambda: away().start())
-            for unit_id in range(2, LAGS[0]):
+            for unit_id in range(1, LAGS[0]):
                 owns[unit_id].start()
                 launch("along", unit_id, along(unit_id))
     own_turn = core == z // 2
+
+    def turn_out(j, half):
+        local, away, stays = turn(j, half)
+        pl.when(stays)(lambda: local().start())
+        pl.when(jnp.logical_not(stays))(lambda: away().start())
+
 
     def small_hop(number):
         landed("small", number - 1)
@@ -552,9 +555,6 @@
         for name in names:
             if name in saves:
                 saves.pop(name).wait()
-
-    def weight(tile):
-        return wbuf[:, :, :, columns(tile)].reshape(1024, TILE)
 
     def norm(layer, which, gain_row, shift_row):
         gain = rows_ref[pl.ds(gain_row, 1)]
@@ -610,102 +610,160 @@
 
         lax.fori_loop(begin, end, body, 0)
 
-    def compute(unit_id):
+    fetched = {}
+
+    def fetch(unit_id):
+        if unit_id < total and unit_id not in fetched:
+            fetched[unit_id] = pltpu.make_async_copy(
+                w_ref.at[unit_id], wbuf.at[unit_id % 2], local_sems.at[2 + unit_id % 2]
+            )
+            fetched[unit_id].start()
+
+    def weight(unit_id, tile):
+        return wbuf[unit_id % 2, :, :, :, columns(tile)].reshape(1024, TILE)
+
+    def project(unit_id):
         layer, kind = unit_id // UNITS, unit_id % UNITS
         base = layer * 12
-        fetch = pltpu.make_async_copy(w_ref.at[unit_id], wbuf, local_sems.at[3])
-        fetch.start()
         if kind == 0:
-            save("low", low, low_ref.at[layer], 0)
-        if kind == 3:
-            heads(layer, 4, 8)
+            settle("qkv")
+        for copy in flying.pop(("kv", (layer - 1, kind)), ()):
+            copy.wait_send()
+
+        def body(tile, carry):
+            value = jnp.dot(low[...], weight(unit_id, tile), preferred_element_type=F32)
+            cols = columns(tile)
+            if kind != 1:
+                value = value + rows_ref[pl.ds(base + kind // 2, 1), cols]
+            value = value.astype(BF)
+            if kind == 0:
+                value = (value.astype(F32) * SCORE_SCALE).astype(BF)
+            qkv[:, columns(tile + 4 * kind)] = value
+            return carry
+
+        lax.fori_loop(0, 4, body, 0)
+        if kind:
+            spot = 6 + 2 * layer + kind - 1
+            src, dst = qkv.at[:, pl.ds(1024 * kind, 1024)], sib.at[layer, kind - 1]
+            launch("kv", (layer, kind), [side(spot, src, dst, here["core"])])
+        if kind == 2:
+            save("qkv", qkv, qkv_ref.at[layer], 1)
+
+    def attention(layer, group):
+        if group == 0:
+            landed("kv", (layer, 1))
+            landed("kv", (layer, 2))
+            save("kv", sib.at[layer], kv_ref.at[layer], 2)
+            settle("mix")
+        heads(layer, 2 * group, 2 * group + 2)
+        if group == 3:
             save("mix", mix, mix_ref.at[layer], 3)
-        fetch.wait()
+
+    def mixing(unit_id):
+        layer = unit_id // UNITS
+        base = layer * 12
+        settle(("unit", 0), ("scale", 0))
+
+        def body(tile, carry):
+            cols = columns(tile)
+            value = jnp.dot(mix[...], weight(unit_id, tile), preferred_element_type=F32)
+            acc[:, cols] = cur[:, cols] + value + rows_ref[pl.ds(base + 2, 1), cols]
+            return carry
+
+        lax.fori_loop(0, 4, body, 0)
+        norm(layer, 0, base + 6, base + 4)
+
+    def widen(unit_id):
+        layer, j = unit_id // UNITS, unit_id % UNITS // 2 - 2
+        base = layer * 12
+        settle(("slope", j))
+
+        def body(tile, carry):
+            cols = columns(tile)
+            value = jnp.dot(nrm[...], weight(unit_id, tile), preferred_element_type=F32)
+            value = value + rows_ref[pl.ds(base + 8 + j, 1), cols]
+            gate = 0.5 * (1.0 + lax.erf(value * 0.7071067811865476))
+            act[j, :, cols] = (value * gate).astype(BF)
+            bell = jnp.exp(-0.5 * value * value)
+            slope[j, :, cols] = (gate + value * (0.3989422804014327 * bell)).astype(BF)
+            return carry
+
+        lax.fori_loop(0, 4, body, 0)
+        save(("slope", j), slope.at[j], slope_ref.at[layer, j], 16 + j)
+
+    def narrow(unit_id):
+        layer, j = unit_id // UNITS, unit_id % UNITS // 2 - 2
+        base = layer * 12
+
+        def body(tile, carry):
+            cols = columns(tile)
+            acc[:, cols] += jnp.dot(act[j], weight(unit_id, tile), preferred_element_type=F32)
+            return carry
+
+        lax.fori_loop(0, 4, body, 0)
+        if j == 3:
+            settle(("unit", 1), ("scale", 1))
+            norm(layer, 1, base + 7, base + 5)
+            if layer == layers - 1:
+                save("low", low, out_ref, 0)
+
+    turns = [0]
+
+    def flip(source, layer, index):
+        slot = turns[0] % 2
+        turns[0] += 1
+        settle(("flip", slot))
+
+        def body(block, carry):
+            for half in range(2):
+                lanes = pl.ds(pl.multiple_of(block * 256 + half * 128, 128), 128)
+                flipped[slot, half, block] = jnp.transpose(source[:, lanes])
+            return carry
+
+        lax.fori_loop(0, 4, body, 0)
+        save(("flip", slot), flipped.at[slot], flip_ref.at[layer, index], 4 + slot)
+
+    chunks = []
+
+    def plan_flip(unit_id, source, index):
+        part = functools.partial(flip, source, unit_id // UNITS, index)
+        chunks.append((unit_id, part, 1.3))
+
+    for unit_id in range(total):
+        layer, kind = unit_id // UNITS, unit_id % UNITS
         if kind < 3:
-            bias = rows_ref[pl.ds(base + (0 if kind == 0 else 1), 1)]
+            chunks.append((unit_id, project, 2.0))
             if kind == 0:
-                settle("qkv")
-            for copy in flying.pop(("kv", (layer - 1, kind)), ()):
-                copy.wait_send()
-
-            def body(tile, carry):
-                value = jnp.dot(low[...], weight(tile), preferred_element_type=F32)
-                cols = columns(tile)
-                if kind != 1:
-                    value = value + rows_ref[pl.ds(base + kind // 2, 1), cols]
-                value = value.astype(BF)
-                if kind == 0:
-                    value = (value.astype(F32) * SCORE_SCALE).astype(BF)
-                qkv[:, columns(tile + 4 * kind)] = value
-                return carry
-
-            lax.fori_loop(0, 4, body, 0)
-            if kind:
-                launch(
-                    "kv",
-                    (layer, kind),
-                    [
-                        side(
-                            6 + 2 * layer + kind - 1,
-                            qkv.at[:, pl.ds(1024 * kind, 1024)],
-                            sib.at[layer, kind - 1],
-                            here["core"],
-                        )
-                    ],
-                )
-            if kind == 2:
-                save("qkv", qkv, qkv_ref.at[layer], 1)
-                landed("kv", (layer, 1))
-                landed("kv", (layer, 2))
-                save("kv", sib.at[layer], kv_ref.at[layer], 2)
-                settle("mix")
-                heads(layer, 0, 4)
+                plan_flip(unit_id, low, 0)
         elif kind == 3:
-            settle("nrm", ("unit", 0), ("scale", 0))
-
-            def body(tile, carry):
-                cols = columns(tile)
-                value = jnp.dot(mix[...], weight(tile), preferred_element_type=F32)
-                acc[:, cols] = cur[:, cols] + value + rows_ref[pl.ds(base + 2, 1), cols]
-                return carry
-
-            lax.fori_loop(0, 4, body, 0)
-            norm(layer, 0, base + 6, base + 4)
-            save("nrm", nrm, nrm_ref.at[layer], 4)
+            for group in range(4):
+                chunks.append((unit_id - 1, functools.partial(attention, layer, group), 4.5))
+            plan_flip(unit_id - 1, mix, 2)
+            chunks.append((unit_id, mixing, 4.5))
+            plan_flip(unit_id, nrm, 1)
         elif kind % 2 == 0:
-            j = kind // 2 - 2
-            settle(("act", j), ("slope", j))
-
-            def body(tile, carry):
-                cols = columns(tile)
-                value = jnp.dot(nrm[...], weight(tile), preferred_element_type=F32)
-                value = value + rows_ref[pl.ds(base + 8 + j, 1), cols]
-                gate = 0.5 * (1.0 + lax.erf(value * 0.7071067811865476))
-                act[j, :, cols] = (value * gate).astype(BF)
-                bell = jnp.exp(-0.5 * value * value)
-                slope[j, :, cols] = (gate + value * (0.3989422804014327 * bell)).astype(BF)
-                return carry
-
-            lax.fori_loop(0, 4, body, 0)
-            save(("act", j), act.at[j], act_ref.at[layer, j], 12 + j)
-            save(("slope", j), slope.at[j], slope_ref.at[layer, j], 16 + j)
+            chunks.append((unit_id, widen, 3.5))
+            plan_flip(unit_id, act.at[kind // 2 - 2], 3 + kind // 2 - 2)
         else:
-            j = kind // 2 - 2
-
-            def body(tile, carry):
-                cols = columns(tile)
-                acc[:, cols] += jnp.dot(act[j], weight(tile), preferred_element_type=F32)
-                return carry
-
-            lax.fori_loop(0, 4, body, 0)
-            if j == 3:
-                settle("low", ("unit", 1), ("scale", 1))
-                norm(layer, 1, base + 7, base + 5)
-                if layer == layers - 1:
-                    save("low", low, out_ref, 0)
+            chunks.append((unit_id, narrow, 5.0 if kind == 11 else 1.5))
+
+    def advance(have, budget):
+        spent = 0.0
+        while chunks and chunks[0][0] <= have and (spent == 0.0 or spent + chunks[0][2] <= budget):
+            unit_id, chunk, cost = chunks.pop(0)
+            if isinstance(chunk, functools.partial):
+                chunk()
+            else:
+                fetch(unit_id)
+                fetched[unit_id].wait()
+                chunk(unit_id)
+                if unit_id + 2 <= have:
+                    fetch(unit_id + 2)
+            spent += cost
 
     ahead, corner_lag, inner_lag, use_lag = LAGS
-    for step in range(total + use_lag):
+    step, have = 0, -1
+    while step < total + use_lag or chunks:
         if step + ahead < total:
             owns[step + ahead].start()
             launch("along", step + ahead, along(step + ahead))
@@ -715,17 +773,27 @@
             launch("across", step, across(step))
         if 0 < step < 4:
             small_hop(step)
+        if step in TURN_STEPS:
+            number = TURN_STEPS.index(step)
+            turn_out(number // 2, number % 2)
+        if step > BEGIN:
+            advance(have, BUDGET)
         if 0 <= step - corner_lag < total:
             landed("across", step - corner_lag)
             launch("corner", step - corner_lag, corner(step - corner_lag))
         if 0 <= step - inner_lag < total:
             landed("corner", step - inner_lag)
             launch("inner", step - inner_lag, inner(step - inner_lag))
-        if step == use_lag:
+        if step == BEGIN:
             begin()
         if 0 <= step - use_lag < total:
             landed("inner", step - use_lag)
-            compute(step - use_lag)
+            have = step - use_lag
+            if have < 2 or have - 2 in fetched and all(item[0] > have - 2 for item in chunks):
+                fetch(have)
+        if step >= BEGIN:
+            advance(have, BUDGET)
+        step += 1
     for j in range(2):
         for half in range(2):
             local, away, stays = turn(j, half)
@@ -747,18 +815,16 @@
     return pl.pallas_call(
         functools.partial(forward_kernel, layers=layers),
         in_specs=[vmem] * 6,
-        out_specs=[any_spec, any_spec, vmem, vmem] + [any_spec] * 9,
+        out_specs=[any_spec, any_spec, vmem, vmem] + [any_spec] * 7,
         out_shape=[
             shape((total, 4, 2, 128, width), BF),
             shape((rows, width), BF),
             shape((layers * 12, width), F32),
             shape((layers, 8, 2, rows), F32),
-            shape((layers, rows, width), BF),
             shape((layers, rows, 3 * width), BF),
             shape((layers, 2, rows, width), BF),
             shape((layers, rows, width), BF),
-            shape((layers, rows, width), BF),
-            shape((layers, 4, rows, width), BF),
+            shape((layers, 7, 2, 4, 128, rows), BF),
             shape((layers, 4, rows, width), BF),
             shape((layers, 2, rows, width), F32),
             shape((layers, 2, rows, 128), F32),
@@ -775,7 +841,8 @@
             pltpu.VMEM((4, rows, width), BF),
             pltpu.VMEM((2, rows, width), F32),
             pltpu.VMEM((2, rows, 128), F32),
-            pltpu.VMEM((4, 2, 128, width), BF),
+            pltpu.VMEM((2, 4, 2, 128, width), BF),
+            pltpu.VMEM((2, 2, 4, 128, rows), BF),
             pltpu.VMEM((total, 32, width), BF),
             pltpu.VMEM((2, 2, 2, 4, layers * 12, 128), F32),
             pltpu.SemaphoreType.DMA((4,)),
@@ -801,12 +868,10 @@
     w_ref,
     rows_ref,
     lse_ref,
-    low_ref,
     qkv_ref,
     kv_ref,
     mix_ref,
-    nrm_ref,
-    act_ref,
+    flip_ref,
     slope_ref,
     unit_ref,
     scale_ref,
@@ -907,15 +972,18 @@
     def rows_of(number, tile):
         return wbuf[number % 2, tile].reshape(TILE, 1024)
 
-    def turn(slot, source):
-        def body(block, carry):
-            rows = pl.ds(pl.multiple_of(block * 128, 128), 128)
-            for half, which in enumerate((core, 1 - core)):
-                lanes = pl.ds(pl.multiple_of(block * 256 + which * 128, 128), 128)
-                turned[slot, half, rows] = jnp.transpose(source[:, lanes])
-            return carry
-
-        lax.fori_loop(0, 4, body, 0)
+    def fetch_turned(slot, layer, index):
+        for half, which in enumerate((core, 1 - core)):
+            fetch(
+                (slot, half),
+                flip_ref.at[layer, index, which],
+                turned.at[slot, half],
+                10 + 2 * slot + half,
+            )
+
+    def ready_turned(slot):
+        ready((slot, 0))
+        ready((slot, 1))
 
     def produce(number, slot, upper):
         buffer = number % 2
@@ -923,7 +991,9 @@
 
         def body(tile, carry):
             cols = columns(tile)
-            value = jnp.dot(turned[slot, 1], upper[:, cols], preferred_element_type=F32)
+            value = jnp.dot(
+                turned[slot, 1].reshape(512, 512), upper[:, cols], preferred_element_type=F32
+            )
             send[buffer, :, :, cols] = value.astype(BF).reshape(4, 128, TILE)
             return carry
 
@@ -932,7 +1002,9 @@
 
         def own(tile, carry):
             cols = columns(tile)
-            value = jnp.dot(turned[slot, 0], upper[:, cols], preferred_element_type=F32)
+            value = jnp.dot(
+                turned[slot, 0].reshape(512, 512), upper[:, cols], preferred_element_type=F32
+            )
             mine[number % slots, :, :, cols] = value.astype(BF).reshape(4, 128, TILE)
             return carry
 
@@ -945,7 +1017,7 @@
         landed("core", number)
 
         def body(block, carry):
-            part[block] = (part[block].astype(F32) + mine[number % slots, block].astype(F32)).astype(BF)
+            part[block] = part[block] + mine[number % slots, block]
             return carry
 
         lax.fori_loop(0, 4, body, 0)
@@ -965,11 +1037,9 @@
         landed("wide", number)
         for block in range(2):
             spot_y = 2 * y + block
-            value = part[spot_y, :, left].astype(F32) + wide[spot, 0, block].astype(F32)
-            part[spot_y, :, left] = value.astype(BF)
+            part[spot_y, :, left] = part[spot_y, :, left] + wide[spot, 0, block]
             spot_x = 2 * block + x
-            value = part[spot_x, :, right].astype(F32) + wide[spot, 1, block].astype(F32)
-            part[spot_x, :, right] = value.astype(BF)
+            part[spot_x, :, right] = part[spot_x, :, right] + wide[spot, 1, block]
         launch(
             "slim",
             number,
@@ -982,8 +1052,8 @@
     def stage_slim(number):
         part, spot = land.at[number % UNITS, 2 * y + x], number % slots
         landed("slim", number)
-        part[:, left] = (part[:, left].astype(F32) + slim[spot, 0].astype(F32)).astype(BF)
-        part[:, right] = (part[:, right].astype(F32) + slim[spot, 1].astype(F32)).astype(BF)
+        part[:, left] = part[:, left] + slim[spot, 0]
+        part[:, right] = part[:, right] + slim[spot, 1]
         copies = []
         for step in (1, 2, 3):
             to = lax.rem(z + step, 4)
@@ -1030,17 +1100,24 @@
     stores = {}
     wide_lag, slim_lag, ends_lag = BACK_LAGS
 
-    def tick():
+    def first_half():
         step = ticks[0]
-        ticks[0] += 1
         if step < total:
             stage_core(step)
         if 0 <= step - wide_lag < total:
             stage_wide(step - wide_lag)
+
+    def second_half():
+        step = ticks[0]
+        ticks[0] += 1
         if 0 <= step - slim_lag < total:
             stage_slim(step - slim_lag)
         if 0 <= step - ends_lag < total:
             stage_ends(step - ends_lag)
+
+    def tick():
+        first_half()
+        second_half()
 
     def norm(base, gain_row, shift_row, sum_row):
         gain = rows_ref[pl.ds(base + gain_row, 1)]
@@ -1079,7 +1156,7 @@
             q = arena[0, :, lanes]
             do = span[:, lanes]
             lane = lax.broadcasted_iota(jnp.int32, q.shape, 1)
-            prod = jnp.transpose(do.astype(F32) * feat[1, :, lanes].astype(F32))
+            prod = jnp.transpose(do.astype(F32) * feat[:, lanes].astype(F32))
             dq = []
             sums = [[None, None], [None, None]]
             for head in range(2):
@@ -1182,26 +1259,22 @@
             fetch_weight(1)
             load_attention(layer)
             ready("top")
-        fetch("act", act_ref.at[layer, 0], arena.at[8], 10)
-        fetch("slope", slope_ref.at[layer, 0], arena.at[9], 11)
-        fetch("nrm", nrm_ref.at[layer], feat.at[0], 12)
-        fetch("mix", mix_ref.at[layer], feat.at[1], 13)
+            fetch_turned(0, layer, 1)
+            fetch_turned(1, layer, 3)
+        fetch("slope", slope_ref.at[layer, 0], arena.at[9], 16)
+        fetch("mix", mix_ref.at[layer], feat, 17)
         first = False
         ready("unit")
         ready("scale")
         norm(base, 7, 5, 3)
         fetch("unit", unit_ref.at[layer, 0], unit, 8)
         fetch("scale", scale_ref.at[layer, 0], scale, 9)
-        ready("nrm")
-        turn(0, feat.at[0])
-        fetch("low", low_ref.at[layer], feat.at[0], 12)
+        ready_turned(0)
         for j in range(4):
             number = start + 2 * j
-            ready("act")
-            turn(1, arena.at[8])
-            if j < 3:
-                fetch("act", act_ref.at[layer, j + 1], arena.at[8], 10)
+            ready_turned(1)
             produce(number, 1, edge)
+            fetch_turned(1, layer, 4 + j if j < 3 else 2)
             ready(("w", number))
             ready("slope")
 
@@ -1220,18 +1293,20 @@
             lax.fori_loop(0, 4, body, 0)
             fetch_weight(number + 2)
             if j < 3:
-                fetch("slope", slope_ref.at[layer, j + 1], arena.at[9], 11)
+                fetch("slope", slope_ref.at[layer, j + 1], arena.at[9], 16)
+            first_half()
             produce(number + 1, 0, span)
             pull(number + 1, span)
-            tick()
+            second_half()
         ready("unit")
         ready("scale")
         norm(base, 6, 4, 2)
         if layer:
             fetch("unit", unit_ref.at[layer - 1, 1], unit, 8)
             fetch("scale", scale_ref.at[layer - 1, 1], scale, 9)
+        fetch_turned(0, layer, 0)
         ready("mix")
-        turn(1, feat.at[1])
+        ready_turned(1)
         number = start + 8
         ready(("w", number))
 
@@ -1243,6 +1318,8 @@
         fetch_weight(number + 2)
         tick()
         produce(number, 1, edge)
+        if layer:
+            fetch_turned(1, layer - 1, 3)
         for part in range(3):
             ready(("qkv", part))
         for part in range(2):
@@ -1259,8 +1336,7 @@
             )
         if layer:
             load_attention(layer - 1)
-        ready("low")
-        turn(0, feat.at[0])
+        ready_turned(0)
         for part in range(3):
             number = start + 9 + part
             if part:
@@ -1268,8 +1344,7 @@
 
                 def body(step, carry):
                     rows = pl.ds(pl.multiple_of(step * 64, 64), 64)
-                    value = arena[5 + part, rows].astype(F32) + arena[9 + part, rows].astype(F32)
-                    arena[5 + part, rows] = value.astype(BF)
+                    arena[5 + part, rows] = arena[5 + part, rows] + arena[9 + part, rows]
                     return carry
 
                 lax.fori_loop(0, 8, body, 0)
@@ -1279,6 +1354,8 @@
             pull(number, arena.at[5 + part])
             if part < 2:
                 tick()
+            elif layer:
+                fetch_turned(0, layer - 1, 1)
         sent("keys", 2 * place)
         sent("keys", 2 * place + 1)
         if layer == 0:
@@ -1365,7 +1442,7 @@
 
 
 def backward_pass(top, last, saved):
-    w, rows, lse, low, qkv, kv, mix, nrm, act, slope, unit, scale = saved
+    w, rows, lse, qkv, kv, mix, flip, slope, unit, scale = saved
     total = w.shape[0]
     layers = total // UNITS
     tokens, width = top.shape
@@ -1374,7 +1451,7 @@
     shape = jax.ShapeDtypeStruct
     return pl.pallas_call(
         functools.partial(backward_kernel, layers=layers),
-        in_specs=[any_spec] * 3 + [vmem, vmem] + [any_spec] * 9,
+        in_specs=[any_spec] * 3 + [vmem, vmem] + [any_spec] * 7,
         out_specs=[any_spec] * 6 + [vmem] * 3,
         out_shape=[
             shape((2, tokens // 2, width), BF),
@@ -1394,8 +1471,8 @@
             pltpu.VMEM((tokens, 128), F32),
             pltpu.VMEM((12, tokens, width), BF),
             pltpu.VMEM((tokens, width), BF),
-            pltpu.VMEM((2, tokens, width), BF),
-            pltpu.VMEM((2, 2, width // 2, tokens), BF),
+            pltpu.VMEM((tokens, width), BF),
+            pltpu.VMEM((2, 2, 4, 128, tokens), BF),
             pltpu.VMEM((2, 4, 2, 128, width), BF),
             pltpu.VMEM((2, 4, 128, width), BF),
             pltpu.VMEM((6, 4, 128, width), BF),
@@ -1407,7 +1484,7 @@
             pltpu.VMEM((10, layers * 12, 128), F32),
             pltpu.VMEM((4, 32, width), F32),
             pltpu.VMEM((32, 4 * width), F32),
-            pltpu.SemaphoreType.DMA((16,)),
+            pltpu.SemaphoreType.DMA((18,)),
             pltpu.SemaphoreType.DMA((5,)),
             pltpu.SemaphoreType.DMA((total, 9)),
             pltpu.SemaphoreType.DMA((total, 9)),
@@ -1418,7 +1495,7 @@
         ],
         compiler_params=pltpu.CompilerParams(has_side_effects=True, vmem_limit_bytes=60 << 20),
         name="backward_pass",
-    )(top, last, w, rows, lse, low, qkv, kv, mix, nrm, act, slope, unit, scale)
+    )(top, last, w, rows, lse, qkv, kv, mix, flip, slope, unit, scale)
 
 
 def swap(value, bit):

time: 571 us -> 539 us (0.944)
  Pallas kernels: 549 us -> 512 us
    pallas_call x1, Pallas kernels: 270 us -> 245 us  [forward_pass(): pl.pallas_call(functools.partial(forward_kernel, layers=layers), in_specs...]
    pallas_call x1, Pallas kernels: 279 us -> 267 us  [backward_pass(): pl.pallas_call(functools.partial(backward_kernel, layers=layers), in_spec...]
  transfers between devices with their start and end apart: 2 -> 2, of which waited for: 0 -> 0; matrix products, arithmetic and copies ran while one was open for 1% -> 1% of each run, Pallas kernels for 48% -> 46%
where the time goes in v2:
time: 539 us; the launch traced here: 536 us
  Pallas kernels  512 us (95%)
  local copies, waits for them, and re-layouts  11.8 us (2%)
    pallas_call x1, Pallas kernels, backward_pass(): pl.pallas_call(functools.partial(backward_kernel, layers=layers), in_spec...  267 us
    pallas_call x1, Pallas kernels, forward_pass(): pl.pallas_call(functools.partial(forward_kernel, layers=layers), in_specs...  245 us
  transfers between devices with their start and end apart: 2, of which 0 were waited for; matrix products, arithmetic and copies ran while one was open for 1% of the time, Pallas kernels for 46%

profile of v2, /device:TPU:0, one launch (start us, length us, event | category | flops | bytes accessed | tf_op | source)
XLA Modules:
  0.0 535.9 jit_solution(11819182743927956933)
XLA Ops:
  0.6 0.0 copy-start
  0.7 0.8 compare_select_fusion
  1.5 0.5 collective-permute-start
  2.0 1.7 constant_dynamic-slice_fusion
  3.7 0.1 copy.35
  3.9 0.1 collective-permute-start.1
  4.0 0.7 copy.27
  4.7 0.1 compare_reduce_fusion
  4.8 0.7 reshape.71
  5.6 0.7 maximum_convert_fusion
  6.3 0.1 tile.9
  6.4 0.0 copy-done
  6.4 2.9 fusion.first_ref
  9.3 0.6 fusion.11.small_ref
  9.9 0.1 add_bitcast_fusion
  10.0 245.2 %forward_pass.1 = (bf16[24,4,2,128,1024]{4,3,2,1,0:T(8,128)(2,1)}, bf16[512,1024]{1,0:T(8,128)(2,1)}, f32[24,1024]{1,0:T(8,128)}, f32[2,8,2,512]{3,2,1,0:T(2,128...) custom-call(bf16[2,256,1024]{2,1,0:T(8,128)(2,1)} %fusion.first_ref,, ...), custom_call_target="tpu_custom_call" | custom-call | tf_op jit(solution)/shard_map/forward_pass/pallas_call | solution.py:815
  255.2 0.0 collective-permute-done
  255.2 0.0 collective-permute-done.1
  255.2 1.8 fusion.2.top_ref
  257.0 267.2 %backward_pass.1 = (bf16[2,256,1024]{2,1,0:T(8,128)(2,1)}, bf16[2,256,1024]{2,1,0:T(8,128)(2,1)}, f32[2,32,3072]{2,1,0:T(8,128)}, f32[2,32,1024]{2,1,0:T(8,128)}...) custom-call(f32[512,1024]{1,0:T(8,128)} %fusion.2.top_ref, ...), custom_call_target="tpu_custom_call" | custom-call | tf_op jit(solution)/shard_map/backward_pass/pallas_call | solution.py:1452
  524.3 0.0 copy-start.4
  524.3 0.0 copy-start.5
  524.3 0.0 copy-start.3
  524.3 1.4 copy.30
  525.8 0.0 copy-start.2
  525.8 0.0 copy-start.1
  525.8 2.9 convert_element_type.29
  528.7 0.0 copy-start.7
  528.7 0.0 copy-start.6
  528.7 2.3 copy.43
  531.0 0.0 copy-done.4
  531.0 0.9 copy.44
  531.8 0.0 copy-done.5
  531.8 0.7 copy.45
  532.5 0.0 copy-done.3
  532.5 1.0 copy.46
  533.5 0.0 copy-done.2
  533.5 1.0 copy.47
  534.5 0.0 copy-done.7
  534.5 0.6 copy.48
  535.1 0.0 copy-done.6
  535.1 0.6 copy.49
  535.6 0.0 copy-done.1
  (11 shorter events, 0.1 us)
Async XLA Ops:
  0.6 5.8 %copy-start = (bf16[2,153,1024]{2,0,1:T(2,128)(2,1)S(1)}, bf16[2,153,1024]{2,0,1:T(2,128)(2,1)}, u32[]{:S(2)}) copy-start(bf16[2,153,1024]{2,0,1:T(2,128)(2,1)} %param.15) | copy-start | bytes 1880068
  1.5 253.7 %collective-permute-start = (f32[153]{0:T(256)S(1)}, f32[153]{0:T(256)S(1)}, u32[]{:S(2)}, u32[]{:S(2)}) collective-permute-start(f32[153]{0:T(256)S(1)} %convert_element_type.24), channel_id=1, source_target_pairs={{0,4},{4,0},{8,12},{12,8},{16,20},{20,16},{24,28},{28,24},{1,5},{5... | collective-permute-start | bytes 1844 | tf_op jit(solution)/shard_map/ppermute | solution.py:1502
  3.9 251.4 %collective-permute-start.1 = (bf16[153,1024]{1,0:T(8,128)(2,1)S(1)}, bf16[153,1024]{1,0:T(8,128)(2,1)S(1)}, u32[]{:S(2)}, u32[]{:S(2)}) collective-permute-start(bf16[153,1024]{1,0:T(8,128)(2,1)S(1)} %bitcast.7), channel_id=1, source_target_pairs={{0,4},{4,0},{8,12},{12,8},{16,20},{20,16},{24,28},{28,24},{1,5},{5... | collective-permute-start | bytes 940040 | tf_op jit(solution)/shard_map/ppermute | solution.py:1502
  524.3 6.7 %copy-start.4 = (f32[2,32,3072]{2,1,0:T(8,128)S(1)}, f32[2,32,3072]{2,1,0:T(8,128)}, u32[]{:S(2)}) copy-start(f32[2,32,3072]{2,1,0:T(8,128)} %get-tuple-element.80) | copy-start | bytes 2359300
  524.3 7.5 %copy-start.5 = (f32[2,32,1024]{2,1,0:T(8,128)S(1)}, f32[2,32,1024]{2,1,0:T(8,128)}, u32[]{:S(2)}) copy-start(f32[2,32,1024]{2,1,0:T(8,128)} %get-tuple-element.81) | copy-start | bytes 786436
  524.3 8.2 %copy-start.3 = (f32[2,32,4096]{2,1,0:T(8,128)S(1)}, f32[2,32,4096]{2,1,0:T(8,128)}, u32[]{:S(2)}) copy-start(f32[2,32,4096]{2,1,0:T(8,128)} %get-tuple-element.82) | copy-start | bytes 3145732
  525.8 7.8 %copy-start.2 = (f32[2,4,32,1024]{3,2,1,0:T(8,128)S(1)}, f32[2,4,32,1024]{3,2,1,0:T(8,128)}, u32[]{:S(2)}) copy-start(f32[2,4,32,1024]{3,2,1,0:T(8,128)} %get-tuple-element.45) | copy-start | bytes 3145732
  525.8 9.9 %copy-start.1 = (bf16[2,153,1024]{2,0,1:T(2,128)(2,1)S(1)}, bf16[2,153,1024]{2,0,1:T(2,128)(2,1)}, u32[]{:S(2)}) copy-start(bf16[2,153,1024]{2,0,1:T(2,128)(2,1)} %param.15) | copy-start | bytes 1880068
  528.7 5.8 %copy-start.7 = (f32[2,128]{1,0:T(2,128)S(1)}, f32[2,128]{1,0:T(2,128)}, u32[]{:S(2)}) copy-start(f32[2,128]{1,0:T(2,128)} %get-tuple-element.85) | copy-start | bytes 3076
  528.7 6.4 %copy-start.6 = (f32[2,2,32]{2,1,0:T(2,128)S(1)}, f32[2,2,32]{2,1,0:T(2,128)}, u32[]{:S(2)}) copy-start(f32[2,2,32]{2,1,0:T(2,128)} %get-tuple-element.86) | copy-start | bytes 1540

commit v3 on v2

--- a/solution.py
+++ b/solution.py
@@ -998,7 +998,7 @@
             return carry
 
         lax.fori_loop(0, 4, body, 0)
-        launch("core", number, [hop(number, 0, send.at[buffer], land.at[number % UNITS], here["core"])])
+        launch("core", number, [hop(number, 0, send.at[buffer], land.at[number % PLACES], here["core"])])
 
         def own(tile, carry):
             cols = columns(tile)
@@ -1012,8 +1012,11 @@
 
     left, right = pl.ds(0, 512), pl.ds(512, 512)
 
+    def chunk_rows(chunk):
+        return pl.ds(pl.multiple_of(chunk * 32, 32), 32)
+
     def stage_core(number):
-        part = land.at[number % UNITS]
+        part = land.at[number % PLACES]
         landed("core", number)
 
         def body(block, carry):
@@ -1033,7 +1036,7 @@
         )
 
     def stage_wide(number):
-        part, spot = land.at[number % UNITS], number % slots
+        part, spot = land.at[number % PLACES], number % slots
         landed("wide", number)
         for block in range(2):
             spot_y = 2 * y + block
@@ -1050,23 +1053,28 @@
         )
 
     def stage_slim(number):
-        part, spot = land.at[number % UNITS, 2 * y + x], number % slots
+        part, spot = land.at[number % PLACES, 2 * y + x], number % slots
         landed("slim", number)
         part[:, left] = part[:, left] + slim[spot, 0]
         part[:, right] = part[:, right] + slim[spot, 1]
         copies = []
-        for step in (1, 2, 3):
-            to = lax.rem(z + step, 4)
-            src = part.at[pl.ds(pl.multiple_of(to * 32, 32), 32)]
-            copies.append(hop(number, 5 + step, src, ends.at[spot, step - 1], (batch, to)))
-        launch("ends", number, copies)
+        for step, chunk in enumerate((z ^ 1, z ^ 3)):
+            copies.append(hop(number, 6 + step, part.at[chunk_rows(chunk)], ends.at[spot, step], (batch, z ^ 1)))
+        launch("pair", number, copies)
+
+    def stage_pair(number):
+        part, spot = land.at[number % PLACES, 2 * y + x], number % slots
+        landed("pair", number)
+        for step, chunk in enumerate((z, z ^ 2)):
+            rows = chunk_rows(chunk)
+            part[rows] = part[rows] + ends[spot, step]
+        src = part.at[chunk_rows(z ^ 2)]
+        launch("ends", number, [hop(number, 8, src, ends.at[spot, 2], (batch, z ^ 2))])
 
     def stage_ends(number):
-        part, spot = land.at[number % UNITS, 2 * y + x], number % slots
+        part, spot = land.at[number % PLACES, 2 * y + x], number % slots
         landed("ends", number)
-        value = part[pl.ds(pl.multiple_of(z * 32, 32), 32)].astype(F32)
-        for step in range(3):
-            value = value + ends[spot, step].astype(F32)
+        value = part[chunk_rows(z)].astype(F32) + ends[spot, 2].astype(F32)
         layer, kind = order[number] // UNITS, order[number] % UNITS
         j = kind // 2 - 2
         if kind > 3 and kind % 2 == 0:
@@ -1093,12 +1101,12 @@
                 dst = out_out.at[layer] if kind == 3 else down_out.at[layer, j]
             stores[slot] = pltpu.make_async_copy(staged.at[slot], dst, store_sems.at[slot])
             stores[slot].start()
-        for kind in ("wide", "slim", "ends"):
+        for kind in ("wide", "slim", "pair", "ends"):
             sent(kind, number)
 
     ticks = [0]
     stores = {}
-    wide_lag, slim_lag, ends_lag = BACK_LAGS
+    wide_lag, slim_lag, pair_lag, ends_lag = BACK_LAGS
 
     def first_half():
         step = ticks[0]
@@ -1112,6 +1120,8 @@
         ticks[0] += 1
         if 0 <= step - slim_lag < total:
             stage_slim(step - slim_lag)
+        if 0 <= step - pair_lag < total:
+            stage_pair(step - pair_lag)
         if 0 <= step - ends_lag < total:
             stage_ends(step - ends_lag)
 
@@ -1438,7 +1448,8 @@
     turn_end(1, edge, grad_out)
 
 
-BACK_LAGS = (2, 4, 5)
+BACK_LAGS = (2, 4, 5, 6)
+PLACES = 13
 
 
 def backward_pass(top, last, saved):
@@ -1476,7 +1487,7 @@
             pltpu.VMEM((2, 4, 2, 128, width), BF),
             pltpu.VMEM((2, 4, 128, width), BF),
             pltpu.VMEM((6, 4, 128, width), BF),
-            pltpu.VMEM((UNITS, 4, 128, width), BF),
+            pltpu.VMEM((PLACES, 4, 128, width), BF),
             pltpu.VMEM((6, 2, 2, 128, width // 2), BF),
             pltpu.VMEM((6, 2, 128, width // 2), BF),
             pltpu.VMEM((6, 3, 32, width), BF),

time: 539 us -> 532 us (0.987)
  Pallas kernels: 512 us -> 505 us
    pallas_call x1, Pallas kernels: 267 us -> 260 us  [backward_pass(): pl.pallas_call(functools.partial(backward_kernel, layers=layers), in_spec...]
where the time goes in v3:
time: 532 us; the launch traced here: 529 us
  Pallas kernels  505 us (95%)
  local copies, waits for them, and re-layouts  11.8 us (2%)
    pallas_call x1, Pallas kernels, backward_pass(): pl.pallas_call(functools.partial(backward_kernel, layers=layers), in_spec...  260 us
    pallas_call x1, Pallas kernels, forward_pass(): pl.pallas_call(functools.partial(forward_kernel, layers=layers), in_specs...  245 us
  transfers between devices with their start and end apart: 2, of which 0 were waited for; matrix products, arithmetic and copies ran while one was open for 1% of the time, Pallas kernels for 46%

profile of v3, /device:TPU:0, one launch (start us, length us, event | category | flops | bytes accessed | tf_op | source)
XLA Modules:
  0.0 528.7 jit_solution(2035514055508353444)
XLA Ops:
  0.6 0.0 copy-start
  0.7 0.8 compare_select_fusion
  1.5 0.5 collective-permute-start
  2.0 1.7 constant_dynamic-slice_fusion
  3.7 0.1 copy.35
  3.9 0.1 collective-permute-start.1
  4.0 0.7 copy.27
  4.7 0.1 compare_reduce_fusion
  4.8 0.7 reshape.71
  5.6 0.7 maximum_convert_fusion
  6.3 0.1 tile.9
  6.4 0.0 copy-done
  6.4 2.9 fusion.first_ref
  9.3 0.6 fusion.11.small_ref
  9.9 0.1 add_bitcast_fusion
  10.0 245.2 %forward_pass.1 = (bf16[24,4,2,128,1024]{4,3,2,1,0:T(8,128)(2,1)}, bf16[512,1024]{1,0:T(8,128)(2,1)}, f32[24,1024]{1,0:T(8,128)}, f32[2,8,2,512]{3,2,1,0:T(2,128...) custom-call(bf16[2,256,1024]{2,1,0:T(8,128)(2,1)} %fusion.first_ref,, ...), custom_call_target="tpu_custom_call" | custom-call | tf_op jit(solution)/shard_map/forward_pass/pallas_call | solution.py:815
  255.2 0.0 collective-permute-done
  255.2 0.0 collective-permute-done.1
  255.2 1.8 fusion.2.top_ref
  257.0 260.0 %backward_pass.1 = (bf16[2,256,1024]{2,1,0:T(8,128)(2,1)}, bf16[2,256,1024]{2,1,0:T(8,128)(2,1)}, f32[2,32,3072]{2,1,0:T(8,128)}, f32[2,32,1024]{2,1,0:T(8,128)}...) custom-call(f32[512,1024]{1,0:T(8,128)} %fusion.2.top_ref, ...), custom_call_target="tpu_custom_call" | custom-call | tf_op jit(solution)/shard_map/backward_pass/pallas_call | solution.py:1463
  517.1 0.0 copy-start.4
  517.1 0.0 copy-start.5
  517.1 0.0 copy-start.3
  517.1 1.4 copy.30
  518.5 0.0 copy-start.2
  518.5 0.0 copy-start.1
  518.5 2.9 convert_element_type.29
  521.5 0.0 copy-start.7
  521.5 0.0 copy-start.6
  521.5 2.3 copy.43
  523.7 0.0 copy-done.4
  523.7 0.9 copy.44
  524.6 0.0 copy-done.5
  524.6 0.7 copy.45
  525.3 0.0 copy-done.3
  525.3 1.0 copy.46
  526.3 0.0 copy-done.2
  526.3 1.0 copy.47
  527.3 0.0 copy-done.7
  527.3 0.6 copy.48
  527.8 0.0 copy-done.6
  527.8 0.6 copy.49
  528.4 0.0 copy-done.1
  (11 shorter events, 0.1 us)
Async XLA Ops:
  0.6 5.8 %copy-start = (bf16[2,153,1024]{2,0,1:T(2,128)(2,1)S(1)}, bf16[2,153,1024]{2,0,1:T(2,128)(2,1)}, u32[]{:S(2)}) copy-start(bf16[2,153,1024]{2,0,1:T(2,128)(2,1)} %param.15) | copy-start | bytes 1880068
  1.5 253.7 %collective-permute-start = (f32[153]{0:T(256)S(1)}, f32[153]{0:T(256)S(1)}, u32[]{:S(2)}, u32[]{:S(2)}) collective-permute-start(f32[153]{0:T(256)S(1)} %convert_element_type.24), channel_id=1, source_target_pairs={{0,4},{4,0},{8,12},{12,8},{16,20},{20,16},{24,28},{28,24},{1,5},{5... | collective-permute-start | bytes 1844 | tf_op jit(solution)/shard_map/ppermute | solution.py:1513
  3.9 251.4 %collective-permute-start.1 = (bf16[153,1024]{1,0:T(8,128)(2,1)S(1)}, bf16[153,1024]{1,0:T(8,128)(2,1)S(1)}, u32[]{:S(2)}, u32[]{:S(2)}) collective-permute-start(bf16[153,1024]{1,0:T(8,128)(2,1)S(1)} %bitcast.7), channel_id=1, source_target_pairs={{0,4},{4,0},{8,12},{12,8},{16,20},{20,16},{24,28},{28,24},{1,5},{5... | collective-permute-start | bytes 940040 | tf_op jit(solution)/shard_map/ppermute | solution.py:1513
  517.1 6.7 %copy-start.4 = (f32[2,32,3072]{2,1,0:T(8,128)S(1)}, f32[2,32,3072]{2,1,0:T(8,128)}, u32[]{:S(2)}) copy-start(f32[2,32,3072]{2,1,0:T(8,128)} %get-tuple-element.80) | copy-start | bytes 2359300
  517.1 7.5 %copy-start.5 = (f32[2,32,1024]{2,1,0:T(8,128)S(1)}, f32[2,32,1024]{2,1,0:T(8,128)}, u32[]{:S(2)}) copy-start(f32[2,32,1024]{2,1,0:T(8,128)} %get-tuple-element.81) | copy-start | bytes 786436
  517.1 8.2 %copy-start.3 = (f32[2,32,4096]{2,1,0:T(8,128)S(1)}, f32[2,32,4096]{2,1,0:T(8,128)}, u32[]{:S(2)}) copy-start(f32[2,32,4096]{2,1,0:T(8,128)} %get-tuple-element.82) | copy-start | bytes 3145732
  518.5 7.8 %copy-start.2 = (f32[2,4,32,1024]{3,2,1,0:T(8,128)S(1)}, f32[2,4,32,1024]{3,2,1,0:T(8,128)}, u32[]{:S(2)}) copy-start(f32[2,4,32,1024]{3,2,1,0:T(8,128)} %get-tuple-element.45) | copy-start | bytes 3145732
  518.5 9.9 %copy-start.1 = (bf16[2,153,1024]{2,0,1:T(2,128)(2,1)S(1)}, bf16[2,153,1024]{2,0,1:T(2,128)(2,1)}, u32[]{:S(2)}) copy-start(bf16[2,153,1024]{2,0,1:T(2,128)(2,1)} %param.15) | copy-start | bytes 1880068
  521.5 5.8 %copy-start.7 = (f32[2,128]{1,0:T(2,128)S(1)}, f32[2,128]{1,0:T(2,128)}, u32[]{:S(2)}) copy-start(f32[2,128]{1,0:T(2,128)} %get-tuple-element.85) | copy-start | bytes 3076
  521.5 6.4 %copy-start.6 = (f32[2,2,32]{2,1,0:T(2,128)S(1)}, f32[2,2,32]{2,1,0:T(2,128)}, u32[]{:S(2)}) copy-start(f32[2,2,32]{2,1,0:T(2,128)} %get-tuple-element.86) | copy-start | bytes 1540

commit v4 on v3

--- a/solution.py
+++ b/solution.py
@@ -1358,10 +1358,10 @@
                     return carry
 
                 lax.fori_loop(0, 8, body, 0)
-            if part != 1:
-                row_sum(base + part // 2, 5 + part)
             produce(number, 0, arena.at[5 + part])
             pull(number, arena.at[5 + part])
+            if part == 0:
+                row_sum(base, 5)
             if part < 2:
                 tick()
             elif layer:
@@ -1377,6 +1377,7 @@
 
             lax.fori_loop(0, 8, body, 0)
             turn_start(1, edge, grad_out)
+        row_sum(base + 1, 7)
         tick()
     base = 2 * layers
 
@@ -1434,12 +1435,13 @@
             for j in range(4):
                 up_bias_out[layer : layer + 1, j * 32 : j * 32 + 32] = mine_row[top + 8 + j : top + 9 + j]
 
-    queue = [small_core, small_y, small_x, small_z, small_end]
+    small_core()
+    queue = [small_y, small_x, small_z, small_end]
     while ticks[0] < total + ends_lag or queue:
+        if ticks[0] < total + ends_lag:
+            tick()
         if queue:
             queue.pop(0)()
-        if ticks[0] < total + ends_lag:
-            tick()
     for kind, number in list(outgoing):
         sent(kind, number)
     for copy in stores.values():

time: 532 us -> 532 us (level)
  no operation moved by 1% of the time
where the time goes in v4:
time: 532 us; the launch traced here: 529 us
  Pallas kernels  506 us (95%)
  local copies, waits for them, and re-layouts  11.8 us (2%)
    pallas_call x1, Pallas kernels, backward_pass(): pl.pallas_call(functools.partial(backward_kernel, layers=layers), in_spec...  260 us
    pallas_call x1, Pallas kernels, forward_pass(): pl.pallas_call(functools.partial(forward_kernel, layers=layers), in_specs...  245 us
  transfers between devices with their start and end apart: 2, of which 0 were waited for; matrix products, arithmetic and copies ran while one was open for 1% of the time, Pallas kernels for 46%

profile of v4, /device:TPU:0, one launch (start us, length us, event | category | flops | bytes accessed | tf_op | source)
XLA Modules:
  0.0 529.0 jit_solution(16564483392673051501)
XLA Ops:
  0.6 0.0 copy-start
  0.7 0.8 compare_select_fusion
  1.5 0.5 collective-permute-start
  2.0 1.7 constant_dynamic-slice_fusion
  3.7 0.1 copy.35
  3.9 0.1 collective-permute-start.1
  4.0 0.7 copy.27
  4.7 0.1 compare_reduce_fusion
  4.8 0.7 reshape.71
  5.6 0.7 maximum_convert_fusion
  6.3 0.1 tile.9
  6.4 0.0 copy-done
  6.4 2.9 fusion.first_ref
  9.3 0.6 fusion.11.small_ref
  9.9 0.1 add_bitcast_fusion
  10.0 245.2 %forward_pass.1 = (bf16[24,4,2,128,1024]{4,3,2,1,0:T(8,128)(2,1)}, bf16[512,1024]{1,0:T(8,128)(2,1)}, f32[24,1024]{1,0:T(8,128)}, f32[2,8,2,512]{3,2,1,0:T(2,128...) custom-call(bf16[2,256,1024]{2,1,0:T(8,128)(2,1)} %fusion.first_ref,, ...), custom_call_target="tpu_custom_call" | custom-call | tf_op jit(solution)/shard_map/forward_pass/pallas_call | solution.py:815
  255.2 0.0 collective-permute-done
  255.2 0.0 collective-permute-done.1
  255.2 1.8 fusion.2.top_ref
  257.0 260.3 %backward_pass.1 = (bf16[2,256,1024]{2,1,0:T(8,128)(2,1)}, bf16[2,256,1024]{2,1,0:T(8,128)(2,1)}, f32[2,32,3072]{2,1,0:T(8,128)}, f32[2,32,1024]{2,1,0:T(8,128)}...) custom-call(f32[512,1024]{1,0:T(8,128)} %fusion.2.top_ref, ...), custom_call_target="tpu_custom_call" | custom-call | tf_op jit(solution)/shard_map/backward_pass/pallas_call | solution.py:1465
  517.4 0.0 copy-start.4
  517.4 0.0 copy-start.5
  517.4 0.0 copy-start.3
  517.4 1.4 copy.30
  518.8 0.0 copy-start.2
  518.8 0.0 copy-start.1
  518.8 2.9 convert_element_type.29
  521.7 0.0 copy-start.7
  521.7 0.0 copy-start.6
  521.7 2.3 copy.43
  524.0 0.0 copy-done.4
  524.0 0.9 copy.44
  524.9 0.0 copy-done.5
  524.9 0.7 copy.45
  525.6 0.0 copy-done.3
  525.6 1.0 copy.46
  526.6 0.0 copy-done.2
  526.6 1.0 copy.47
  527.5 0.0 copy-done.7
  527.5 0.6 copy.48
  528.1 0.0 copy-done.6
  528.1 0.6 copy.49
  528.7 0.0 copy-done.1
  (11 shorter events, 0.1 us)
Async XLA Ops:
  0.6 5.8 %copy-start = (bf16[2,153,1024]{2,0,1:T(2,128)(2,1)S(1)}, bf16[2,153,1024]{2,0,1:T(2,128)(2,1)}, u32[]{:S(2)}) copy-start(bf16[2,153,1024]{2,0,1:T(2,128)(2,1)} %param.15) | copy-start | bytes 1880068
  1.5 253.7 %collective-permute-start = (f32[153]{0:T(256)S(1)}, f32[153]{0:T(256)S(1)}, u32[]{:S(2)}, u32[]{:S(2)}) collective-permute-start(f32[153]{0:T(256)S(1)} %convert_element_type.24), channel_id=1, source_target_pairs={{0,4},{4,0},{8,12},{12,8},{16,20},{20,16},{24,28},{28,24},{1,5},{5... | collective-permute-start | bytes 1844 | tf_op jit(solution)/shard_map/ppermute | solution.py:1515
  3.9 251.4 %collective-permute-start.1 = (bf16[153,1024]{1,0:T(8,128)(2,1)S(1)}, bf16[153,1024]{1,0:T(8,128)(2,1)S(1)}, u32[]{:S(2)}, u32[]{:S(2)}) collective-permute-start(bf16[153,1024]{1,0:T(8,128)(2,1)S(1)} %bitcast.7), channel_id=1, source_target_pairs={{0,4},{4,0},{8,12},{12,8},{16,20},{20,16},{24,28},{28,24},{1,5},{5... | collective-permute-start | bytes 940040 | tf_op jit(solution)/shard_map/ppermute | solution.py:1515
  517.4 6.7 %copy-start.4 = (f32[2,32,3072]{2,1,0:T(8,128)S(1)}, f32[2,32,3072]{2,1,0:T(8,128)}, u32[]{:S(2)}) copy-start(f32[2,32,3072]{2,1,0:T(8,128)} %get-tuple-element.80) | copy-start | bytes 2359300
  517.4 7.5 %copy-start.5 = (f32[2,32,1024]{2,1,0:T(8,128)S(1)}, f32[2,32,1024]{2,1,0:T(8,128)}, u32[]{:S(2)}) copy-start(f32[2,32,1024]{2,1,0:T(8,128)} %get-tuple-element.81) | copy-start | bytes 786436
  517.4 8.2 %copy-start.3 = (f32[2,32,4096]{2,1,0:T(8,128)S(1)}, f32[2,32,4096]{2,1,0:T(8,128)}, u32[]{:S(2)}) copy-start(f32[2,32,4096]{2,1,0:T(8,128)} %get-tuple-element.82) | copy-start | bytes 3145732
  518.8 7.8 %copy-start.2 = (f32[2,4,32,1024]{3,2,1,0:T(8,128)S(1)}, f32[2,4,32,1024]{3,2,1,0:T(8,128)}, u32[]{:S(2)}) copy-start(f32[2,4,32,1024]{3,2,1,0:T(8,128)} %get-tuple-element.45) | copy-start | bytes 3145732
  518.8 9.9 %copy-start.1 = (bf16[2,153,1024]{2,0,1:T(2,128)(2,1)S(1)}, bf16[2,153,1024]{2,0,1:T(2,128)(2,1)}, u32[]{:S(2)}) copy-start(bf16[2,153,1024]{2,0,1:T(2,128)(2,1)} %param.15) | copy-start | bytes 1880068
  521.7 5.8 %copy-start.7 = (f32[2,128]{1,0:T(2,128)S(1)}, f32[2,128]{1,0:T(2,128)}, u32[]{:S(2)}) copy-start(f32[2,128]{1,0:T(2,128)} %get-tuple-element.85) | copy-start | bytes 3076
  521.7 6.4 %copy-start.6 = (f32[2,2,32]{2,1,0:T(2,128)S(1)}, f32[2,2,32]{2,1,0:T(2,128)}, u32[]{:S(2)}) copy-start(f32[2,2,32]{2,1,0:T(2,128)} %get-tuple-element.86) | copy-start | bytes 1540
